TPU v7x, 32 devices: a whole 2x2x4 slice. The times are simulated.
32 devices in a mesh: row: 4 (over y, x), col: 8 (over z, core).
Axes of the slice: x: 2, y: 2, z: 4, core: 2. Of those that a mesh axis runs over, the one named last changes fastest.
Arguments:
- parent_front: bfloat16 [28672, 28672], P('row', 'col'), may hold values from -6 to 6
- child_update: bfloat16 [2, 14336, 14336], P(None, 'row', 'col'), may hold values from -6 to 6
- parent_test: bfloat16 [28672, 448], P('col'), may hold values from -0.03125 to 0.03125
- child_test: bfloat16 [2, 14336, 448], P(None, 'col'), may hold values from -0.046875 to 0.046875
- child_map: int32 [2, 112], replicated, may hold values from 0 to 223, as said below
Outputs:
- leaf_basis: bfloat16 [224, 128, 448], P('row', 'col')
- couplings: float32 [32, 448, 448], P('row', 'col')
Inputs may be any that keep to these rules, and one draw needn't show every extreme that they name: `child_map`: for each child the entries rise strictly along its blocks, and entry j is at least j.
All inputs are finite; a program needn't handle non-finite values.
Results may differ from a plain program's by a relative error of at most 0.006.
Values may be sent and summed in bfloat16 or wider, within the bound.
A program may use at most 192 MiB of HBM per device.

v0:
```python
import functools
import math

import jax
import jax.numpy as jnp
from jax import lax
from jax.experimental import pallas as pl
from jax.experimental.pallas import tpu as pltpu
from jax.sharding import PartitionSpec as P


LEAF = 896
BLOCK = 128
PIVOTS = 64
GROUP = 4

HIGH = lax.Precision.HIGHEST
MESH = pl.DeviceIdType.MESH


def dot(a, b, dims):
    return lax.dot_general(
        a, b, (dims, ((), ())), precision=HIGH, preferred_element_type=jnp.float32
    )


def inverse_factor(tile, nb):
    ridx = lax.broadcasted_iota(jnp.int32, tile.shape, 0)
    lane = lax.broadcasted_iota(jnp.int32, tile.shape, 1)
    for j in range(0, nb, GROUP):
        cols = [
            jnp.broadcast_to(tile[:, nb + j + k : nb + j + k + 1], tile.shape)
            for k in range(GROUP)
        ]
        rows = [tile[j + k : j + k + 1, :] for k in range(GROUP)]
        for k in range(GROUP):
            at = j + k
            factor = jnp.where(ridx > at, cols[k] * (1.0 / cols[k][at : at + 1, :]), 0.0)
            for m in range(k + 1, GROUP):
                cols[m] = cols[m] - factor * cols[m][at : at + 1, :]
                rows[m] = rows[m] - factor[j + m : j + m + 1, :] * rows[k]
            cols[k] = factor
        for k in range(GROUP):
            tile = tile - cols[k] * rows[k]
    pivots = jnp.sum(jnp.where(lane == ridx + nb, tile, 0.0), axis=1, keepdims=True)
    return tile[:, :nb] * lax.rsqrt(pivots)


def basis_kernel(scale, yt_ref, qt_ref, gram_ref, work_ref):
    nb = PIVOTS
    probes = yt_ref.shape[0]
    work_ref[...] = yt_ref[...]
    gram_ref[...] = dot(yt_ref[...], yt_ref[...], ((1,), (1,)))

    def step(index, carry):
        start = pl.multiple_of(index * nb, nb)
        panel = gram_ref[pl.ds(start, nb), :]
        source = lax.broadcasted_iota(jnp.int32, (probes, 2 * nb), 0)
        lane = lax.broadcasted_iota(jnp.int32, (probes, 2 * nb), 1)
        pick = jnp.where((lane >= nb) & (source == lane - nb + start), 1.0, 0.0)
        eye = jnp.where(
            lax.broadcasted_iota(jnp.int32, (nb, 2 * nb), 0)
            == lax.broadcasted_iota(jnp.int32, (nb, 2 * nb), 1),
            1.0,
            0.0,
        )
        inverse = inverse_factor(dot(panel, pick, ((1,), (0,))) + eye, nb)
        top = dot(inverse, panel, ((1,), (0,)))
        solved = dot(inverse, work_ref[pl.ds(start, nb), :], ((1,), (0,)))
        qt_ref[pl.ds(start, nb), :] = (solved * scale).astype(qt_ref.dtype)
        gram_ref[...] -= dot(top, top, ((0,), (0,)))
        work_ref[...] -= dot(top, solved, ((0,), (0,)))
        return carry

    lax.fori_loop(0, probes // nb, step, 0)


def leaf_basis_of(yt):
    probes, rows = yt.shape
    return pl.pallas_call(
        functools.partial(basis_kernel, math.sqrt(LEAF)),
        out_shape=jax.ShapeDtypeStruct((probes, rows), jnp.bfloat16),
        in_specs=[pl.BlockSpec(memory_space=pltpu.VMEM)],
        out_specs=pl.BlockSpec(memory_space=pltpu.VMEM),
        scratch_shapes=[
            pltpu.VMEM((probes, probes), jnp.float32),
            pltpu.VMEM((probes, rows), jnp.float32),
        ],
        compiler_params=pltpu.CompilerParams(vmem_limit_bytes=40 << 20),
        cost_estimate=pl.CostEstimate(
            flops=40 * probes * probes * rows,
            bytes_accessed=6 * probes * rows,
            transcendentals=0,
        ),
        name="leaf_basis",
    )(yt)


def probe_kernel(parity_ref, front_ref, test_ref, kept_ref, sent_ref):
    total = jnp.dot(front_ref[...], test_ref[...], preferred_element_type=jnp.float32)
    blocks, pairs, slab, probes = kept_ref.shape
    view = total.reshape(blocks * pairs, 2, slab, probes)
    even = parity_ref[0] == 0
    kept_ref[...] = jnp.where(even, view[:, 0], view[:, 1]).reshape(kept_ref.shape)
    sent_ref[...] = jnp.where(even, view[:, 1], view[:, 0]).reshape(sent_ref.shape)


def probe(front, test, which, first_row, rows, col_count, parity):
    depth, probes = test.shape[1:]
    tile = max(t for t in range(BLOCK, 4 * BLOCK + 1, BLOCK) if rows % t == 0)
    pairs, slab = col_count // 2, BLOCK // col_count
    half = jax.ShapeDtypeStruct((rows // BLOCK, pairs, slab, probes), jnp.float32)
    out_spec = pl.BlockSpec((tile // BLOCK, pairs, slab, probes), lambda i, p: (i, 0, 0, 0))
    skip = first_row // tile
    return pl.pallas_call(
        probe_kernel,
        out_shape=(half, half),
        grid_spec=pltpu.PrefetchScalarGridSpec(
            num_scalar_prefetch=1,
            grid=(rows // tile,),
            in_specs=[
                pl.BlockSpec((None, tile, depth), lambda i, p: (which, skip + i, 0)),
                pl.BlockSpec((None, depth, probes), lambda i, p: (which, 0, 0)),
            ],
            out_specs=(out_spec, out_spec),
        ),
        compiler_params=pltpu.CompilerParams(vmem_limit_bytes=40 << 20),
        cost_estimate=pl.CostEstimate(
            flops=2 * rows * depth * probes,
            bytes_accessed=2 * rows * depth + 2 * depth * probes + 4 * rows * probes,
            transcendentals=0,
        ),
        name="probe",
    )(parity, front, test)


def swap_pair(halves, col_count):
    kept, sent = halves
    return kept, lax.ppermute(sent, "col", [(c, c ^ 1) for c in range(col_count)])


def send_pairs(kept, swapped, col_count, pair_index):
    pairs = col_count // 2

    def piece(pair):
        return lax.dynamic_index_in_dim(kept, pair, 1, False) + lax.dynamic_index_in_dim(
            swapped, pair, 1, False
        )

    came = [
        lax.ppermute(
            piece((pair_index + shift) % pairs).astype(jnp.bfloat16),
            "col",
            [(c, (c + 2 * shift) % col_count) for c in range(col_count)],
        )
        for shift in range(1, pairs)
    ]
    return piece(pair_index), came


def add_up(own, came):
    for term in came:
        own = own + term.astype(jnp.float32)
    return own


def spread(total, parts, grain):
    base = total // grain
    cuts = [base * (i + 1) // parts * grain for i in range(parts)]
    starts = [0] + cuts[:-1]
    return [(s, e - s) for s, e in zip(starts, cuts)]


def sample_kernel(
    dims,
    picks_ref,
    kid_test_hbm,
    test_hbm,
    kids_hbm,
    front_hbm,
    yt_ref,
    kid_test,
    test,
    ring,
    parts,
    kid_sum,
    sums,
    kid_in,
    kid_in_two,
    came,
    came_two,
    kids,
    merged,
    landed,
    load_sem,
    test_sem,
    swap_send,
    swap_recv,
    kid_send,
    kid_recv,
    kid_recv_two,
    line_send,
    line_recv,
    line_recv_two,
    row_send,
    row_recv,
    leaf_send,
    leaf_recv,
):
    row_count, col_count, kid_tiles, kid_each, order, slots, subs = dims
    chips = col_count // 2
    probes, rows = yt_ref.shape
    half = probes // 2
    per_leaf = rows // BLOCK
    blocks = merged.shape[0]
    pieces = slots
    row, col = lax.axis_index("row"), lax.axis_index("col")
    chip, core = col // 2, col % 2
    sibling = {"col": chip * 2 + 1 - core}

    def remote(src, dst, send, recv, target):
        return pltpu.make_async_remote_copy(
            src_ref=src, dst_ref=dst, send_sem=send, recv_sem=recv,
            device_id=target, device_id_type=MESH,
        )

    barrier = pltpu.get_barrier_semaphore()
    for shift in range(1, col_count):
        pl.semaphore_signal(
            barrier, inc=1, device_id={"col": (col + shift) % col_count}, device_id_type=MESH
        )
    for shift in range(1, row_count):
        pl.semaphore_signal(
            barrier, inc=1, device_id={"row": (row + shift) % row_count}, device_id_type=MESH
        )

    kid_depth = kid_test.shape[2]

    def pair_at(at):
        return jnp.where(at % 2 == 0, chips - 1 - at // 2, at // 2)

    def load_kid(index):
        index = jnp.asarray(index, jnp.int32)
        start = pl.multiple_of(index % kid_each * rows, rows)
        return pltpu.make_async_copy(
            kids_hbm.at[index // kid_each, pl.ds(start, rows)],
            ring.at[index % 2, :, pl.ds(0, kid_depth)],
            load_sem.at[index % 2],
        )

    def load_front(index):
        index = jnp.asarray(index, jnp.int32)
        leaf = 2 * pair_at(index // 2) + jnp.where(index % 2 == 0, 1 - core, core)
        return pltpu.make_async_copy(
            front_hbm.at[pl.ds(pl.multiple_of(leaf * rows, rows), rows)],
            ring.at[index % 2],
            load_sem.at[index % 2],
        )

    kid_test_load = pltpu.make_async_copy(kid_test_hbm, kid_test, test_sem.at[0])
    test_load = pltpu.make_async_copy(test_hbm, test, test_sem.at[1])
    load_kid(0).start()
    kid_test_load.start()
    load_kid(1).start()
    test_load.start()
    kid_test_load.wait()

    def product(left, right):
        return lax.dot_general(
            left, right, (((1,), (1,)), ((), ())), preferred_element_type=jnp.float32
        )

    def kid_swap(tile):
        away = pl.ds(pl.multiple_of((1 - core) * half, half), half)
        return remote(
            parts.at[tile % 4, away], kid_sum.at[tile],
            swap_send.at[tile], swap_recv.at[tile], sibling,
        )

    def swap(at):
        return remote(
            parts.at[2 * at % 4], sums.at[pair_at(at)],
            swap_send.at[kid_tiles + at], swap_recv.at[kid_tiles + at], sibling,
        )

    def kid_combine(tile):
        kid_swap(tile).wait_recv()
        own = pl.ds(pl.multiple_of(core * half, half), half)
        kid_sum[tile] += parts[tile % 4, own]

    def combine(at):
        swap(at).wait_recv()
        sums[pair_at(at)] += parts[(2 * at + 1) % 4]

    def kid_hop(tile, goal, right, last, target):
        start, size = pieces[goal]
        span = pl.ds(start, size)
        two = last and not right
        dst = kid_in_two.at[tile, pl.ds(0, size)] if two else kid_in.at[tile, span]
        sem = kid_recv_two.at[tile] if two else kid_recv.at[tile, goal]
        return remote(
            kid_in.at[tile, span], dst, kid_send.at[tile, goal], sem, {"col": target}
        )

    def kid_push(tile, goal, here):
        start, size = pieces[goal]
        span = pl.ds(start, size)
        right = goal > here
        last = goal == here + 1 if right else goal == here - 1
        kid_in[tile, span] = kid_sum[tile, span].astype(jnp.bfloat16)
        kid_hop(tile, goal, right, last, col + 2 if right else col - 2).start()

    def kid_take(tile, goal, here, right):
        start, size = pieces[goal]
        span = pl.ds(start, size)
        last = goal == here
        kid_hop(tile, goal, right, last, col - 2 if right else col + 2).wait_recv()
        if last and not right:
            kid_sum[tile, span] += kid_in_two[tile, :size].astype(jnp.float32)
        else:
            kid_sum[tile, span] += kid_in[tile, span].astype(jnp.float32)

    def kid_share(tile, shift, here, toward=1):
        size = pieces[here][1]
        other = (row + toward * shift + row_count) % row_count
        owner = row if toward == 1 else other
        span = kids.at[pl.ds(owner * blocks + tile * per_leaf, per_leaf), pl.ds(0, size)]
        return remote(
            span, span, row_send.at[tile, shift - 1], row_recv.at[tile, shift - 1],
            {"row": other},
        )

    def on_chip(here, body):
        pl.when(chip == here)(body)

    def each_chip(body):
        for here in range(chips):
            on_chip(here, functools.partial(body, here))

    end = chips - 1

    def kid_head(tile):
        def right():
            for goal in reversed(range(1, chips)):
                kid_push(tile, goal, 0)

        def left():
            for goal in range(end):
                kid_push(tile, goal, end)

        on_chip(0, right)
        on_chip(end, left)

    def kid_stage(stage, tile):
        def right():
            for goal in reversed(range(stage + 1, chips)):
                kid_take(tile, goal, stage, True)
                kid_push(tile, goal, stage)

        def left():
            for goal in range(end - stage):
                kid_take(tile, goal, end - stage, False)
                kid_push(tile, goal, end - stage)

        def final(here):
            if here > 0:
                kid_take(tile, here, here, True)
            if here < end:
                kid_take(tile, here, here, False)
            start, size = pieces[here]
            for block in range(per_leaf):
                kids[row * blocks + tile * per_leaf + block, :size] = kid_sum[
                    tile, start : start + size, block * BLOCK : (block + 1) * BLOCK
                ]
            for shift in range(1, row_count):
                kid_share(tile, shift, here).start()

        if stage < end:
            on_chip(stage, right)
            on_chip(end - stage, left)
        for here in range(chips):
            if max(here, end - here) == stage:
                on_chip(here, functools.partial(final, here))

    sub = probes // subs

    def hop(pair, piece, right, last, target):
        span = pl.ds(pl.multiple_of(piece * sub, sub), sub)
        two = last and not right
        dst = came_two.at[span] if two else came.at[pair, span]
        sem = line_recv_two.at[piece] if two else line_recv.at[pair, piece]
        return remote(
            came.at[pair, span], dst, line_send.at[pair, piece], sem, {"col": target}
        )

    def push(pair, piece, here):
        span = pl.ds(pl.multiple_of(piece * sub, sub), sub)
        right = pair > here
        last = pair == here + 1 if right else pair == here - 1
        came[pair, span] = sums[pair, span].astype(jnp.bfloat16)
        hop(pair, piece, right, last, col + 2 if right else col - 2).start()

    def take(pair, piece, here, right):
        span = pl.ds(pl.multiple_of(piece * sub, sub), sub)
        last = pair == here
        hop(pair, piece, right, last, col - 2 if right else col + 2).wait_recv()
        if last and not right:
            sums[pair, span] += came_two[span].astype(jnp.float32)
        else:
            sums[pair, span] += came[pair, span].astype(jnp.float32)

    def head(pair, here):
        def body():
            def one(piece, carry):
                push(pair, piece, here)
                return carry

            lax.fori_loop(0, subs, one, 0)

        on_chip(here, body)

    def stage_of(stage, pair, piece):
        def right():
            take(pair, piece, stage, True)
            push(pair, piece, stage)

        def left():
            take(pair, piece, end - stage, False)
            push(pair, piece, end - stage)

        def final():
            if pair > 0:
                take(pair, piece, pair, True)
            if pair < end:
                take(pair, piece, pair, False)

        if pair > stage and stage < end:
            on_chip(stage, right)
        if pair < end - stage and stage < end:
            on_chip(end - stage, left)
        if max(pair, end - pair) == stage:
            on_chip(pair, final)

    def chain(pairs):
        deepest = max(max(pair, end - pair) for pair in pairs)

        def one(turn, carry):
            for stage in range(1, deepest + 1):
                at = turn - (stage - 1)

                @pl.when((at >= 0) & (at < subs))
                def _(stage=stage, at=at):
                    for pair in pairs:
                        stage_of(stage, pair, at)

            return carry

        lax.fori_loop(0, subs + deepest - 1, one, 0)

    kids[row_count * blocks] = jnp.zeros(kids.shape[1:], kids.dtype)

    def kid_turn(tile, carry):
        pl.when(tile >= 4)(lambda: kid_swap(tile - 4).wait_send())
        load_kid(tile).wait()
        parts[tile % 4] = product(kid_test[tile // kid_each], ring[tile % 2, :, :kid_depth])
        pl.when(tile + 2 < kid_tiles)(lambda: load_kid(tile + 2).start())
        pl.when(tile + 2 >= kid_tiles)(lambda: load_front(tile + 2 - kid_tiles).start())

        @pl.when(tile == 0)
        def _():
            pl.semaphore_wait(barrier, col_count - 1 + row_count - 1)

        kid_swap(tile).start()

        @pl.when(tile > 0)
        def _():
            kid_combine(tile - 1)
            kid_head(tile - 1)

        return carry

    lax.fori_loop(0, kid_tiles, kid_turn, 0)
    test_load.wait()
    turns = 2 * chips

    def turn_of(index, carry):
        at = index // 2

        @pl.when(index < 4)
        def _():
            kid_swap(kid_tiles + index - 4).wait_send()

        @pl.when((index >= 4) & (index % 2 == 0))
        def _():
            swap(at - 2).wait_send()

        load_front(index).wait()
        parts[index % 4] = product(test[...], ring[index % 2])
        pl.when(index + 2 < turns)(lambda: load_front(index + 2).start())

        @pl.when(index % 2 == 0)
        def _():
            swap(at).start()

        @pl.when(index == 0)
        def _():
            kid_combine(kid_tiles - 1)
            kid_head(kid_tiles - 1)

        @pl.when((index % 2 == 0) & (index > 0))
        def _():
            combine(at - 1)

        for spot in range(chips - 1):

            @pl.when(index == 2 * spot + 2)
            def _(spot=spot):
                if order[spot] > 0:
                    head(order[spot], 0)
                if order[spot] < end and spot < chips - 2:
                    head(order[spot], end)

        for stage in range(1, chips):
            tile = index - (stage - 1)
            pl.when((tile >= 0) & (tile < kid_tiles))(
                functools.partial(kid_stage, stage, tile)
            )
        return carry

    lax.fori_loop(0, turns, turn_of, 0)
    combine(chips - 1)
    if order[-1] > 0:
        head(order[-1], 0)
    for pair in (order[-1], order[-2]):
        if pair < end:
            head(pair, end)

    def tail_turn(index, carry):
        for stage in range(1, chips):
            tile = index - (stage - 1)
            pl.when((tile >= 0) & (tile < kid_tiles))(
                functools.partial(kid_stage, stage, tile)
            )
        return carry

    lax.fori_loop(turns, kid_tiles + chips - 2, tail_turn, 0)
    chain(order[:2])
    chain(order[2:])

    def leaf_move(shift, here):
        size = pieces[here][1]
        goal = (col + shift) % col_count
        return remote(
            merged.at[pl.ds(goal * per_leaf, per_leaf), pl.ds(0, size)],
            landed.at[col, :, pl.ds(0, size)],
            leaf_send.at[shift - 1], leaf_recv.at[shift - 1], {"col": goal},
        )

    def merge(here):
        size = pieces[here][1]

        def arrive(tile, carry):
            for shift in range(1, row_count):
                kid_share(tile, shift, here, -1).wait_recv()
            return carry

        lax.fori_loop(0, kid_tiles, arrive, 0)

        def one(block, carry):
            first = kids[picks_ref[0, block], :size]
            second = kids[picks_ref[1, block], :size]
            merged[block, :size] = (first + second).astype(jnp.bfloat16)
            return carry

        lax.fori_loop(0, blocks, one, 0)
        for shift in range(1, col_count):
            leaf_move(shift, here).start()
        landed[col, :, :size] = merged[pl.ds(col * per_leaf, per_leaf), :size]

    each_chip(merge)

    def land():
        for shift in range(1, col_count):
            source = (col - shift + col_count) % col_count
            far = source // 2
            for there in range(chips):

                def wait(there=there):
                    size = pieces[there][1]
                    remote(
                        merged.at[pl.ds(0, per_leaf), pl.ds(0, size)],
                        landed.at[source, :, pl.ds(0, size)],
                        leaf_send.at[shift - 1], leaf_recv.at[shift - 1], {"col": source},
                    ).wait_recv()

                pl.when(far == there)(wait)

    land()
    for source in range(col_count):
        start, size = pieces[source // 2]
        start += source % 2 * half
        for block in range(per_leaf):
            lanes = pl.ds(block * BLOCK, BLOCK)
            yt_ref[pl.ds(start, size), lanes] = (
                sums[chip, pl.ds(start, size), lanes]
                + landed[source, block, :size].astype(jnp.float32)
            )

    def drain(here):
        def one(tile, carry):
            for goal in range(chips):
                if goal != here:
                    kid_hop(tile, goal, goal > here, False, col).wait_send()
            for shift in range(1, row_count):
                kid_share(tile, shift, here).wait_send()
            return carry

        lax.fori_loop(0, kid_tiles, one, 0)
        for pair in range(chips):
            if pair != here:
                for piece in range(subs):
                    hop(pair, piece, pair > here, False, col).wait_send()
        for shift in range(1, col_count):
            leaf_move(shift, here).wait_send()

    each_chip(drain)
    for at in range(chips - 2, chips):
        swap(at).wait_send()


def sample_of(picks, kid_test, test, kids, front, row_count, col_count):
    depth = front.shape[1]
    probes = test.shape[0]
    kid_rows, kid_depth = kids.shape[1:]
    chips = col_count // 2
    half = probes // 2
    kid_each = kid_rows // LEAF
    kid_tiles = kids.shape[0] * kid_each
    per_leaf = LEAF // BLOCK
    blocks = front.shape[0] // BLOCK
    subs = 4
    pieces = spread(half, chips, 16)
    most = max(size for _, size in pieces)
    low, high, order = 0, chips - 1, []
    while low <= high:
        order += [high] if low == high else [high, low]
        low, high = low + 1, high - 1
    f32, bf16 = jnp.float32, jnp.bfloat16
    dims = (row_count, col_count, kid_tiles, kid_each, tuple(order), tuple(pieces), subs)
    any_spec = pl.BlockSpec(memory_space=pl.ANY)
    dma = pltpu.SemaphoreType.DMA
    return pl.pallas_call(
        functools.partial(sample_kernel, dims),
        out_shape=jax.ShapeDtypeStruct((probes, LEAF), f32),
        in_specs=[pl.BlockSpec(memory_space=pltpu.SMEM)] + [any_spec] * 4,
        out_specs=pl.BlockSpec(memory_space=pltpu.VMEM),
        scratch_shapes=[
            pltpu.VMEM((kids.shape[0], probes, kid_depth), bf16),
            pltpu.VMEM((probes, depth), bf16),
            pltpu.VMEM((2, LEAF, depth), bf16),
            pltpu.VMEM((4, probes, LEAF), f32),
            pltpu.VMEM((kid_tiles, half, LEAF), f32),
            pltpu.VMEM((chips, probes, LEAF), f32),
            pltpu.VMEM((kid_tiles, half, LEAF), bf16),
            pltpu.VMEM((kid_tiles, most, LEAF), bf16),
            pltpu.VMEM((chips, probes, LEAF), bf16),
            pltpu.VMEM((probes, LEAF), bf16),
            pltpu.VMEM((row_count * blocks + 1, most, BLOCK), f32),
            pltpu.VMEM((blocks, most, BLOCK), bf16),
            pltpu.VMEM((col_count, per_leaf, most, BLOCK), bf16),
            dma((2,)),
            dma((2,)),
            dma((kid_tiles + chips,)),
            dma((kid_tiles + chips,)),
            dma((kid_tiles, chips)),
            dma((kid_tiles, chips)),
            dma((kid_tiles,)),
            dma((chips, subs)),
            dma((chips, subs)),
            dma((subs,)),
            dma((kid_tiles, row_count - 1)),
            dma((kid_tiles, row_count - 1)),
            dma((col_count - 1,)),
            dma((col_count - 1,)),
        ],
        compiler_params=pltpu.CompilerParams(
            collective_id=0, has_side_effects=True, vmem_limit_bytes=67043328
        ),
        cost_estimate=pl.CostEstimate(
            flops=4 * front.shape[0] * depth * probes,
            bytes_accessed=4 * front.shape[0] * depth,
            transcendentals=0,
        ),
        name="sample",
    )(picks, kid_test, test, kids, front)


def finish_kernel(
    dims,
    yt_ref,
    front_hbm,
    basis_ref,
    core_ref,
    gram,
    work,
    exact,
    high,
    low,
    near_high,
    near_low,
    far,
    tile,
    slab,
    slab_in,
    stage,
    stage_in,
    tile_send,
    tile_recv,
    near_send,
    near_recv,
    far_send,
    far_recv,
    slab_send,
    slab_recv,
    core_send,
    core_recv,
):
    _, col_count, tile_leaves = dims
    nb = PIVOTS
    chips = col_count // 2
    probes, rows = yt_ref.shape
    per_leaf = rows // BLOCK
    rank_rows = probes // col_count
    groups = slab.shape[0]
    steps = probes // nb
    scale = math.sqrt(LEAF)
    shrink = 1.0 / scale
    row, col = lax.axis_index("row"), lax.axis_index("col")
    chip, core = col // 2, col % 2
    sibling = {"col": chip * 2 + 1 - core}
    at_home = chip == row

    def far_of(pair):
        return (pair >= row + 2) | (pair + 2 <= row)

    def remote(src, dst, send, recv, target):
        return pltpu.make_async_remote_copy(
            src_ref=src, dst_ref=dst, send_sem=send, recv_sem=recv,
            device_id=target, device_id_type=MESH,
        )

    barrier = pltpu.get_barrier_semaphore()
    for shift in range(1, col_count):
        pl.semaphore_signal(
            barrier, inc=1, device_id={"col": (col + shift) % col_count}, device_id_type=MESH
        )
    pl.semaphore_wait(barrier, col_count - 1)

    def tile_source(position):
        slot = core * tile_leaves + (position ^ 1)
        return front_hbm.at[
            pl.ds(pl.multiple_of(slot * rows, rows), rows), pl.ds(position * rows, rows)
        ]

    def each_tile(act):
        for position in range(tile_leaves):
            parity = (position ^ 1) % 2
            pair = (core * tile_leaves + (position ^ 1)) // 2
            slot = pair * 2 + parity
            is_far = far_of(pair)
            goal = jnp.where(is_far, 2 * row + pair % 2, slot)
            for place, chosen in ((0, jnp.logical_not(is_far)), (1 + parity, is_far)):
                here = at_home & chosen & (goal == col)
                there = at_home & chosen & (goal != col)

                def stay(place=place, position=position):
                    act(
                        pltpu.make_async_copy(
                            tile_source(position), tile.at[place], tile_recv.at[place]
                        ),
                        False,
                    )

                def go(place=place, position=position, goal=goal):
                    act(
                        remote(
                            tile_source(position), tile.at[place], tile_send.at[position],
                            tile_recv.at[place], {"col": goal},
                        ),
                        True,
                    )

                pl.when(here)(stay)
                pl.when(there)(go)

    each_tile(lambda copy, away: copy.start())

    work[...] = yt_ref[...]
    gram[...] = dot(yt_ref[...], yt_ref[...], ((1,), (1,)))

    def near_copy(step, which):
        span = pl.ds(pl.multiple_of(step * nb, nb), nb)
        src, dst = ((high, near_high), (low, near_low))[which]
        return remote(
            src.at[span], dst.at[span], near_send.at[which, step], near_recv.at[which, step],
            sibling,
        )

    def far_copy(step, parity):
        span = pl.ds(pl.multiple_of(step * nb, nb), nb)
        return remote(
            high.at[span], far.at[parity, span], far_send.at[step], far_recv.at[parity, step],
            {"col": 2 * row + chip % 2},
        )

    def slab_copy(group, shift, toward=1):
        other = (col + toward * shift + col_count) % col_count
        owner = col if toward == 1 else other
        return remote(
            slab.at[group, other], slab_in.at[group, owner],
            slab_send.at[group, shift], slab_recv.at[group, shift], {"col": other},
        )

    per_slab = BLOCK // col_count

    def send_slabs(group, count):
        start = pl.multiple_of(group * BLOCK, BLOCK)
        for block in range(per_leaf):
            turned = exact[pl.ds(start, count), block * BLOCK : (block + 1) * BLOCK].T
            for goal in range(col_count):
                slab[group, goal, block, :, :count] = turned[
                    goal * per_slab : (goal + 1) * per_slab
                ].astype(slab.dtype)
        for shift in range(1, col_count):
            slab_copy(group, shift).start()
        slab_in[group, col] = slab[group, col]

    def step(index, carry):
        start = pl.multiple_of(index * nb, nb)
        panel = gram[pl.ds(start, nb), :]
        source = lax.broadcasted_iota(jnp.int32, (probes, 2 * nb), 0)
        lane = lax.broadcasted_iota(jnp.int32, (probes, 2 * nb), 1)
        pick = jnp.where((lane >= nb) & (source == lane - nb + start), 1.0, 0.0)
        eye = jnp.where(
            lax.broadcasted_iota(jnp.int32, (nb, 2 * nb), 0)
            == lax.broadcasted_iota(jnp.int32, (nb, 2 * nb), 1),
            1.0,
            0.0,
        )
        inverse = inverse_factor(dot(panel, pick, ((1,), (0,))) + eye, nb)
        top = dot(inverse, panel, ((1,), (0,)))
        solved = dot(inverse, work[pl.ds(start, nb), :], ((1,), (0,)))
        scaled = solved * scale
        rounded = scaled.astype(high.dtype)
        exact[pl.ds(start, nb), :] = scaled
        high[pl.ds(start, nb), :] = rounded
        low[pl.ds(start, nb), :] = (scaled - rounded.astype(jnp.float32)).astype(low.dtype)
        gram[...] -= dot(top, top, ((0,), (0,)))
        work[...] -= dot(top, solved, ((0,), (0,)))

        @pl.when(far_of(chip))
        def _():
            for parity in range(2):
                pl.when(core == parity)(lambda parity=parity: far_copy(index, parity).start())

        @pl.when(jnp.logical_not(far_of(chip)))
        def _():
            near_copy(index, 0).start()
            near_copy(index, 1).start()

        @pl.when(index % 2 == 1)
        def _():
            send_slabs(index // 2, BLOCK)

        return carry

    lax.fori_loop(0, steps, step, 0)
    if steps % 2 == 1:
        send_slabs(groups - 1, nb)

    def times(a, b):
        return lax.dot_general(
            a, b, (((1,), (1,)), ((), ())), preferred_element_type=jnp.float32
        )

    def core_copy(place, goal, slot):
        return remote(
            stage.at[place, goal], stage_in.at[slot], core_send.at[place, goal],
            core_recv.at[slot], {"col": goal},
        )

    def send_core(place, slot, value):
        value = (value * shrink).astype(stage.dtype)
        for goal in range(col_count):
            stage[place, goal, :rank_rows] = value[goal * rank_rows : (goal + 1) * rank_rows]

            @pl.when(goal != col)
            def _(goal=goal):
                core_copy(place, goal, slot).start()

            @pl.when(goal == col)
            def _(goal=goal):
                stage_in[slot] = stage[place, goal]

    def wait_tile(place, source):
        @pl.when(source == col)
        def _():
            pltpu.make_async_copy(
                front_hbm.at[pl.ds(0, rows), pl.ds(0, rows)], tile.at[place],
                tile_recv.at[place],
            ).wait()

        @pl.when(source != col)
        def _():
            remote(
                front_hbm.at[pl.ds(0, rows), pl.ds(0, rows)], tile.at[place], tile_send.at[0],
                tile_recv.at[place], {"col": source},
            ).wait_recv()

    @pl.when(jnp.logical_not(far_of(chip)))
    def _():
        wait_tile(0, 2 * row + col // tile_leaves)
        for index in range(steps):
            near_copy(index, 0).wait_recv()
            near_copy(index, 1).wait_recv()
        product = (times(near_high[...], tile[0]) + times(near_low[...], tile[0])) * shrink
        rounded = product.astype(jnp.bfloat16)
        rest = (product - rounded.astype(jnp.float32)).astype(jnp.bfloat16)
        send_core(
            0, col,
            times(high[...], rounded) + (times(low[...], rounded) + times(high[...], rest)),
        )

    for pair in range(chips):

        @pl.when(at_home & far_of(pair) & (core == pair % 2))
        def _(pair=pair):
            for parity in range(2):
                for index in range(steps):
                    span = pl.ds(index * nb, nb)
                    remote(
                        high.at[span], far.at[parity, span], far_send.at[index],
                        far_recv.at[parity, index], {"col": 2 * pair + parity},
                    ).wait_recv()
            for parity in range(2):
                slot = 2 * pair + parity
                wait_tile(1 + parity, 2 * row + slot // tile_leaves)
                product = times(far[1 - parity], tile[1 + parity]) * shrink
                send_core(1 + parity, slot, times(far[parity], product.astype(jnp.bfloat16)))

    for group in range(groups):
        for shift in range(1, col_count):
            slab_copy(group, shift, -1).wait_recv()
    for slot in range(col_count):
        for group in range(groups):
            count = min(BLOCK, probes - group * BLOCK)
            basis_ref[
                slot * per_leaf : (slot + 1) * per_leaf, :, group * BLOCK : group * BLOCK + count
            ] = slab_in[group, slot, :, :, :count]
    for slot in range(col_count):
        pair = slot // 2
        source = jnp.where(far_of(pair), 2 * row + pair % 2, slot)

        @pl.when(source != col)
        def _(slot=slot, source=source):
            remote(
                stage.at[0, 0], stage_in.at[slot], core_send.at[0, 0], core_recv.at[slot],
                {"col": source},
            ).wait_recv()

        core_ref[slot] = stage_in[slot, :rank_rows].astype(jnp.float32)

    def settle(copy, away):
        if away:
            copy.wait_send()

    each_tile(settle)

    @pl.when(far_of(chip))
    def _():
        for index in range(steps):
            far_copy(index, 0).wait_send()

    @pl.when(jnp.logical_not(far_of(chip)))
    def _():
        for index in range(steps):
            near_copy(index, 0).wait_send()
            near_copy(index, 1).wait_send()
        for goal in range(col_count):
            pl.when(goal != col)(lambda goal=goal: core_copy(0, goal, col).wait_send())

    for group in range(groups):
        for shift in range(1, col_count):
            slab_copy(group, shift).wait_send()
    for pair in range(chips):

        @pl.when(at_home & far_of(pair) & (core == pair % 2))
        def _(pair=pair):
            for parity in range(2):
                for goal in range(col_count):
                    pl.when(goal != col)(
                        lambda goal=goal, parity=parity: core_copy(
                            1 + parity, goal, 2 * pair + parity
                        ).wait_send()
                    )


def finish(yt, front, row_count, col_count):
    probes, rows = yt.shape
    steps = probes // PIVOTS
    per_leaf = rows // BLOCK
    blocks = front.shape[0] // BLOCK
    groups = -(-probes // BLOCK)
    rank_rows = probes // col_count
    padded = -(-rank_rows // 16) * 16
    f32, bf16 = jnp.float32, jnp.bfloat16
    dma = pltpu.SemaphoreType.DMA
    slab = pltpu.VMEM((groups, col_count, per_leaf, BLOCK // col_count, BLOCK), bf16)
    dims = (row_count, col_count, front.shape[1] // LEAF)
    return pl.pallas_call(
        functools.partial(finish_kernel, dims),
        out_shape=(
            jax.ShapeDtypeStruct((blocks, BLOCK // col_count, probes), bf16),
            jax.ShapeDtypeStruct((col_count, rank_rows, probes), f32),
        ),
        in_specs=[
            pl.BlockSpec(memory_space=pltpu.VMEM),
            pl.BlockSpec(memory_space=pl.ANY),
        ],
        out_specs=(
            pl.BlockSpec(memory_space=pltpu.VMEM),
            pl.BlockSpec(memory_space=pltpu.VMEM),
        ),
        scratch_shapes=[
            pltpu.VMEM((probes, probes), f32),
            pltpu.VMEM((probes, rows), f32),
            pltpu.VMEM((probes, rows), f32),
            pltpu.VMEM((probes, rows), bf16),
            pltpu.VMEM((probes, rows), bf16),
            pltpu.VMEM((probes, rows), bf16),
            pltpu.VMEM((probes, rows), bf16),
            pltpu.VMEM((2, probes, rows), bf16),
            pltpu.VMEM((3, rows, rows), bf16),
            slab,
            slab,
            pltpu.VMEM((3, col_count, padded, probes), bf16),
            pltpu.VMEM((col_count, padded, probes), bf16),
            dma((dims[2],)),
            dma((3,)),
            dma((2, steps)),
            dma((2, steps)),
            dma((steps,)),
            dma((2, steps)),
            dma((groups, col_count)),
            dma((groups, col_count)),
            dma((3, col_count)),
            dma((col_count,)),
        ],
        compiler_params=pltpu.CompilerParams(
            collective_id=1, has_side_effects=True, vmem_limit_bytes=56 << 20
        ),
        cost_estimate=pl.CostEstimate(
            flops=40 * probes * probes * rows,
            bytes_accessed=6 * probes * rows,
            transcendentals=0,
        ),
        name="finish",
    )(yt, front)


def general(parent_front, child_update, parent_test, child_test, child_map):
    row_count = lax.axis_size("row")
    col_count = lax.axis_size("col")
    row_index = lax.axis_index("row")
    col_index = lax.axis_index("col")
    slab = BLOCK // col_count
    own_blocks = parent_front.shape[0] // BLOCK
    probes = parent_test.shape[1]
    per_leaf = LEAF // BLOCK
    leaf_count = own_blocks // per_leaf
    col_leaves = parent_front.shape[1] // LEAF
    shrink = 1.0 / math.sqrt(LEAF)

    tie = lax.optimization_barrier
    pair_index = col_index // 2
    parity = col_index % 2
    half = own_blocks // 2 * BLOCK
    sign = jnp.reshape(parity, (1,)).astype(jnp.int32)
    fronts, tests = parent_front[None], parent_test[None]
    kid_rows = child_update.shape[1]

    def send_tile(position, front):
        sibling = col_index * col_leaves + position
        row_start = jnp.bitwise_xor(sibling, 1) % leaf_count * LEAF
        tile = lax.dynamic_slice(front, (row_start, position * LEAF), (LEAF, LEAF))
        routes = []
        for row in range(row_count):
            for slot in range(leaf_count):
                other = (row * leaf_count + slot) ^ 1
                if other % col_leaves == position:
                    routes.append(
                        (row * col_count + other // col_leaves, row * col_count + slot)
                    )
        return lax.ppermute(tile, ("row", "col"), routes)

    pieces = {position: send_tile(position, parent_front) for position in range(0, col_leaves, 2)}

    jobs = (
        (child_update, child_test, 0, 0, kid_rows),
        (child_update, child_test, 1, 0, kid_rows),
        (fronts, tests, 0, 0, half),
        (fronts, tests, 0, half, half),
    )
    sums = []
    for front, test, which, first_row, rows in jobs:
        halves = probe(front, test, which, first_row, rows, col_count, sign)
        kept, swapped = swap_pair(halves, col_count)
        sums.append(send_pairs(kept, swapped, col_count, pair_index))
    (first_own, first_came), (second_own, second_came) = sums[:2]
    (upper_own, upper_came), (lower_own, lower_came) = sums[2:]

    kid_share = jnp.stack([add_up(first_own, first_came), add_up(second_own, second_came)])
    all_kids = lax.all_gather(kid_share, "row", axis=1, tiled=True)
    own_share = jnp.concatenate([add_up(upper_own, upper_came), add_up(lower_own, lower_came)])

    targets = jnp.arange(own_blocks, dtype=jnp.int32)
    mapped = child_map - row_index * own_blocks
    onehot = (mapped[:, None, :] == targets[None, :, None]).astype(jnp.float32)
    sample = own_share + jnp.einsum("cpn,cnsr->psr", onehot, all_kids, precision=HIGH)

    by_leaf = sample.reshape(leaf_count, per_leaf * slab, probes)
    by_leaf = jnp.pad(by_leaf, ((0, col_count - leaf_count), (0, 0), (0, 0)))
    leaf_rows = lax.all_to_all(by_leaf, "col", 0, 0, tiled=True).reshape(LEAF, probes)

    leaf_rows, front = tie((leaf_rows, parent_front))
    for position in range(1, col_leaves, 2):
        pieces[position] = send_tile(position, front)
    wanted = jnp.bitwise_xor(col_index, 1) % col_leaves
    front_tile = pieces[0]
    for position in range(1, col_leaves):
        front_tile = jnp.where(wanted == position, pieces[position], front_tile)

    basis_t = leaf_basis_of(leaf_rows.T)
    basis = basis_t.T
    slabs = lax.all_to_all(
        basis.reshape(col_count, per_leaf * slab, probes), "col", 0, 0, tiled=True
    )
    leaf_basis = slabs[:leaf_count].reshape(own_blocks, slab, probes)

    natural = (
        basis.reshape(col_count, per_leaf, slab, probes)
        .transpose(1, 0, 2, 3)
        .reshape(LEAF, probes)
    )
    sibling_basis = lax.ppermute(natural, "col", [(c, c ^ 1) for c in range(col_count)])
    product = jnp.dot(front_tile, sibling_basis, preferred_element_type=jnp.float32) * shrink
    core = (
        lax.dot_general(
            natural,
            product.astype(jnp.bfloat16),
            (((0,), (0,)), ((), ())),
            preferred_element_type=jnp.float32,
        )
        * shrink
    )
    cores = lax.all_to_all(
        core.reshape(col_count, probes // col_count, probes), "col", 0, 0, tiled=True
    )
    return (leaf_basis, cores[:leaf_count])


def fits(parent_front, child_update, row_count, col_count):
    leaf_count = parent_front.shape[0] // LEAF
    return (
        leaf_count == col_count
        and row_count * 2 == col_count
        and child_update.shape[0] * child_update.shape[1] // LEAF % 4 == 0
        and all(
            sum(abs(pair - row) > 1 and pair % 2 == core for pair in range(row_count)) < 2
            for row in range(row_count)
            for core in range(2)
        )
        and parent_front.shape[1] // LEAF * 2 == leaf_count
        and col_count % 2 == 0
        and parent_front.shape[1] % LEAF == 0
        and child_update.shape[1] % LEAF == 0
        and 2 * parent_front.shape[1] * LEAF * 2 < 16 << 20
    )


def picks_of(child_map, row_index, row_count, own_blocks):
    kid_count, kid_blocks = child_map.shape
    each = kid_blocks // row_count
    at = jnp.arange(kid_blocks, dtype=jnp.int32)
    which = jnp.arange(kid_count, dtype=jnp.int32)
    value = (at // each * own_blocks + at % each)[None, :] + which[:, None] * each
    targets = jnp.arange(own_blocks, dtype=jnp.int32)
    match = (child_map - row_index * own_blocks)[:, None, :] == targets[None, :, None]
    found = jnp.max(jnp.where(match, value[:, None, :], -1), axis=2)
    return jnp.where(found < 0, row_count * own_blocks, found)


def local(parent_front, child_update, parent_test, child_test, child_map):
    row_count = lax.axis_size("row")
    col_count = lax.axis_size("col")
    if not fits(parent_front, child_update, row_count, col_count):
        return general(parent_front, child_update, parent_test, child_test, child_map)
    row_index = lax.axis_index("row")
    own_blocks = parent_front.shape[0] // BLOCK
    picks = picks_of(child_map, row_index, row_count, own_blocks)
    yt = sample_of(
        picks, child_test.transpose(0, 2, 1), parent_test.T, child_update, parent_front,
        row_count, col_count,
    )
    return tuple(finish(yt, parent_front, row_count, col_count))


def solution(mesh):
    in_specs = (P("row", "col"), P(None, "row", "col"), P("col", None), P(None, "col", None), P())
    out_specs = (P("row", "col", None), P("row", "col", None))
    return jax.shard_map(local, mesh=mesh, in_specs=in_specs, out_specs=out_specs, check_vma=False)
```

profile of v0, /device:TPU:0, one launch (start us, length us, event | category | flops | bytes accessed | tf_op | source)
XLA Modules:
  0.0 226.7 jit_solution(8261735146257991775)
XLA Ops:
  0.7 0.8 broadcast_add_fusion
  1.4 0.1 select_reduce_fusion
  1.5 0.6 compare_select_fusion.picks_ref
  2.1 131.8 %sample.1.yt_ref = f32[448,896]{1,0:T(8,128)} custom-call(s32[2,56]{1,0:T(2,128)} %compare_select_fusion.picks_ref, bf16[2,448,1792]{2,1,0:T(8,128)(2,1)} %bitcast.2, bf16[448,3584]{1,0:T(8,128)(2,1)} %bitcast.3, bf16[2,3584,1792]{2,1,0:T(8,128)(2,1)} %kids_hbm.1, bf16[7168,3584]{1,0:T(8,128)(2,1)} %front_hbm.3), custom_call_target="tpu_custom_call" | custom-call | flops 46036680704 | bytes 102760448 | tf_op jit(solution)/shard_map/sample/pallas_call | solution.py:652
  133.9 88.5 %finish.1 = (bf16[56,16,448]{2,1,0:T(8,128)(2,1)}, f32[8,56,448]{2,1,0:T(8,128)}) custom-call(f32[448,896]{1,0:T(8,128)} %sample.1.yt_ref, bf16[7168,3584]{1,0:T(8,128)(2,1)} %front_hbm.3), custom_call_target="tpu_custom_call" | custom-call | flops 7193231360 | bytes 2408448 | tf_op jit(solution)/shard_map/finish/pallas_call | solution.py:1020
  222.4 2.2 copy.9
  224.6 2.2 copy.10
  (2 shorter events, 0.0 us)
where the time goes:
time: 227 us
  Pallas kernels  220 us (97%)
  local copies, waits for them, and re-layouts  4.32 us (2%)
    pallas_call x1, Pallas kernels, sample_of(): pl.pallas_call(functools.partial(sample_kernel, dims), out_shape=jax.Shap...  132 us
    pallas_call x1, Pallas kernels, finish(): pl.pallas_call(functools.partial(finish_kernel, dims), out_shape=(jax.Sha...  88.5 us

commit v1 on v0

--- a/solution.py
+++ b/solution.py
@@ -12,7 +12,7 @@
 LEAF = 896
 BLOCK = 128
 PIVOTS = 64
-GROUP = 4
+GROUP = 8
 
 HIGH = lax.Precision.HIGHEST
 MESH = pl.DeviceIdType.MESH
@@ -695,6 +695,29 @@
     )(picks, kid_test, test, kids, front)
 
 
+def parts_of(x):
+    high = x.astype(jnp.bfloat16).astype(jnp.float32)
+    rest = x - high
+    middle = rest.astype(jnp.bfloat16).astype(jnp.float32)
+    return high, middle, rest - middle
+
+
+def left_parts(x, axis):
+    high, middle, low = parts_of(x)
+    stacked = jnp.concatenate([high, high, middle, middle, high, low], axis=axis)
+    return stacked.astype(jnp.bfloat16)
+
+
+def right_parts(x):
+    high, middle, low = parts_of(x)
+    stacked = jnp.concatenate([high, middle, high, middle, low, high], axis=0)
+    return stacked.astype(jnp.bfloat16)
+
+
+def fast_dot(a, b, dims):
+    return lax.dot_general(a, b, (dims, ((), ())), preferred_element_type=jnp.float32)
+
+
 def finish_kernel(
     dims,
     yt_ref,
@@ -796,7 +819,14 @@
     each_tile(lambda copy, away: copy.start())
 
     work[...] = yt_ref[...]
-    gram[...] = dot(yt_ref[...], yt_ref[...], ((1,), (1,)))
+    one, two, three = (part.astype(jnp.bfloat16) for part in parts_of(yt_ref[...]))
+    both = ((1,), (1,))
+    small = fast_dot(two, two, both) + fast_dot(one, three, both) + fast_dot(three, one, both)
+    middle = fast_dot(one, two, both) + fast_dot(two, one, both)
+    wide = gram.shape[1]
+    gram[:, :probes] = fast_dot(one, one, both) + (middle + small)
+    if wide > probes:
+        gram[:, probes:] = jnp.zeros((probes, wide - probes), jnp.float32)
 
     def near_copy(step, which):
         span = pl.ds(pl.multiple_of(step * nb, nb), nb)
@@ -832,31 +862,29 @@
                     goal * per_slab : (goal + 1) * per_slab
                 ].astype(slab.dtype)
         for shift in range(1, col_count):
-            slab_copy(group, shift).start()
+            ready = jnp.logical_not(far_of(chip) & ((col + shift) % col_count // 2 == row))
+            pl.when(ready)(lambda shift=shift: slab_copy(group, shift).start())
         slab_in[group, col] = slab[group, col]
 
     def step(index, carry):
         start = pl.multiple_of(index * nb, nb)
         panel = gram[pl.ds(start, nb), :]
-        source = lax.broadcasted_iota(jnp.int32, (probes, 2 * nb), 0)
-        lane = lax.broadcasted_iota(jnp.int32, (probes, 2 * nb), 1)
-        pick = jnp.where((lane >= nb) & (source == lane - nb + start), 1.0, 0.0)
-        eye = jnp.where(
-            lax.broadcasted_iota(jnp.int32, (nb, 2 * nb), 0)
-            == lax.broadcasted_iota(jnp.int32, (nb, 2 * nb), 1),
-            1.0,
-            0.0,
-        )
-        inverse = inverse_factor(dot(panel, pick, ((1,), (0,))) + eye, nb)
-        top = dot(inverse, panel, ((1,), (0,)))
-        solved = dot(inverse, work[pl.ds(start, nb), :], ((1,), (0,)))
+        square = gram[pl.ds(start, nb), pl.ds(pl.multiple_of(index // 2 * 2 * nb, 2 * nb), 2 * nb)]
+        square = jnp.where(index % 2 == 0, pltpu.roll(square, nb, 1), square)
+        lane = lax.broadcasted_iota(jnp.int32, square.shape, 1)
+        eye = jnp.where(lax.broadcasted_iota(jnp.int32, square.shape, 0) == lane, 1.0, 0.0)
+        inverse = inverse_factor(jnp.where(lane >= nb, square, eye), nb)
+        inverse_parts = left_parts(inverse, 1)
+        top = fast_dot(inverse_parts, right_parts(panel), ((1,), (0,)))
+        solved = fast_dot(inverse_parts, right_parts(work[pl.ds(start, nb), :]), ((1,), (0,)))
         scaled = solved * scale
         rounded = scaled.astype(high.dtype)
         exact[pl.ds(start, nb), :] = scaled
         high[pl.ds(start, nb), :] = rounded
         low[pl.ds(start, nb), :] = (scaled - rounded.astype(jnp.float32)).astype(low.dtype)
-        gram[...] -= dot(top, top, ((0,), (0,)))
-        work[...] -= dot(top, solved, ((0,), (0,)))
+        top_parts = left_parts(top[:, :probes], 0)
+        gram[...] -= fast_dot(top_parts, right_parts(top), ((0,), (0,)))
+        work[...] -= fast_dot(top_parts, right_parts(solved), ((0,), (0,)))
 
         @pl.when(far_of(chip))
         def _():
@@ -877,6 +905,13 @@
     lax.fori_loop(0, steps, step, 0)
     if steps % 2 == 1:
         send_slabs(groups - 1, nb)
+    for shift in range(1, col_count):
+
+        @pl.when(far_of(chip) & ((col + shift) % col_count // 2 == row))
+        def _(shift=shift):
+            for group in range(groups):
+                slab_copy(group, shift).start()
+
 
     def times(a, b):
         return lax.dot_general(
@@ -1032,7 +1067,7 @@
             pl.BlockSpec(memory_space=pltpu.VMEM),
         ),
         scratch_shapes=[
-            pltpu.VMEM((probes, probes), f32),
+            pltpu.VMEM((probes, groups * BLOCK), f32),
             pltpu.VMEM((probes, rows), f32),
             pltpu.VMEM((probes, rows), f32),
             pltpu.VMEM((probes, rows), bf16),
@@ -1183,6 +1218,7 @@
         and parent_front.shape[1] // LEAF * 2 == leaf_count
         and col_count % 2 == 0
         and parent_front.shape[1] % LEAF == 0
+        and 2 * PIVOTS == BLOCK
         and child_update.shape[1] % LEAF == 0
         and 2 * parent_front.shape[1] * LEAF * 2 < 16 << 20
     )

time: 227 us -> 227 us (level)
  no operation moved by 1% of the time
where the time goes in v1:
time: 227 us
  Pallas kernels  220 us (97%)
  local copies, waits for them, and re-layouts  4.32 us (2%)
    pallas_call x1, Pallas kernels, sample_of(): pl.pallas_call(functools.partial(sample_kernel, dims), out_shape=jax.Shap...  132 us
    pallas_call x1, Pallas kernels, finish(): pl.pallas_call(functools.partial(finish_kernel, dims), out_shape=(jax.Sha...  88.5 us

profile of v1, /device:TPU:0, one launch (start us, length us, event | category | flops | bytes accessed | tf_op | source)
XLA Modules:
  0.0 226.7 jit_solution(15782120095164800315)
XLA Ops:
  0.7 0.8 broadcast_add_fusion
  1.4 0.1 select_reduce_fusion
  1.5 0.6 compare_select_fusion.picks_ref
  2.1 131.8 %sample.1.yt_ref = f32[448,896]{1,0:T(8,128)} custom-call(s32[2,56]{1,0:T(2,128)} %compare_select_fusion.picks_ref, bf16[2,448,1792]{2,1,0:T(8,128)(2,1)} %bitcast.2, bf16[448,3584]{1,0:T(8,128)(2,1)} %bitcast.3, bf16[2,3584,1792]{2,1,0:T(8,128)(2,1)} %kids_hbm.1, bf16[7168,3584]{1,0:T(8,128)(2,1)} %front_hbm.3), custom_call_target="tpu_custom_call" | custom-call | flops 46036680704 | bytes 102760448 | tf_op jit(solution)/shard_map/sample/pallas_call | solution.py:652
  133.9 88.5 %finish.1 = (bf16[56,16,448]{2,1,0:T(8,128)(2,1)}, f32[8,56,448]{2,1,0:T(8,128)}) custom-call(f32[448,896]{1,0:T(8,128)} %sample.1.yt_ref, bf16[7168,3584]{1,0:T(8,128)(2,1)} %front_hbm.3), custom_call_target="tpu_custom_call" | custom-call | flops 7193231360 | bytes 2408448 | tf_op jit(solution)/shard_map/finish/pallas_call | solution.py:1055
  222.4 2.2 copy.9
  224.6 2.2 copy.10
  (2 shorter events, 0.0 us)

commit v2 on v0

--- a/solution.py
+++ b/solution.py
@@ -12,7 +12,7 @@
 LEAF = 896
 BLOCK = 128
 PIVOTS = 64
-GROUP = 4
+GROUP = 8
 
 HIGH = lax.Precision.HIGHEST
 MESH = pl.DeviceIdType.MESH
@@ -164,6 +164,335 @@
     return own
 
 
+def parts_of(x):
+    high = x.astype(jnp.bfloat16).astype(jnp.float32)
+    rest = x - high
+    middle = rest.astype(jnp.bfloat16).astype(jnp.float32)
+    return high, middle, rest - middle
+
+
+def left_parts(x, axis):
+    high, middle, low = parts_of(x)
+    stacked = jnp.concatenate([high, high, middle, middle, high, low], axis=axis)
+    return stacked.astype(jnp.bfloat16)
+
+
+def right_parts(x):
+    high, middle, low = parts_of(x)
+    stacked = jnp.concatenate([high, middle, high, middle, low, high], axis=0)
+    return stacked.astype(jnp.bfloat16)
+
+
+def fast_dot(a, b, dims):
+    return lax.dot_general(a, b, (dims, ((), ())), preferred_element_type=jnp.float32)
+
+
+def finishing(
+    dims, tile_at, far_at, front_hbm, basis_ref, core_ref, gram, work, exact, high, low,
+    near_high, near_low, slab, slab_in, stage, stage_in, sems,
+):
+    groups, _, slab_rows, _ = slab_in.shape
+
+    (
+        tile_send, tile_recv, near_send, near_recv, far_send, far_recv, slab_send, slab_recv,
+        core_send, core_recv,
+    ) = sems
+    _, col_count, tile_leaves = dims
+    nb = PIVOTS
+    chips = col_count // 2
+    probes, rows = work.shape
+    per_leaf = rows // BLOCK
+    rank_rows = probes // col_count
+    steps = probes // nb
+    scale = math.sqrt(LEAF)
+    shrink = 1.0 / scale
+    row, col = lax.axis_index("row"), lax.axis_index("col")
+    chip, core = col // 2, col % 2
+    sibling = {"col": chip * 2 + 1 - core}
+    at_home = chip == row
+
+    def far_of(pair):
+        return (pair >= row + 2) | (pair + 2 <= row)
+
+    def remote(src, dst, send, recv, target):
+        return pltpu.make_async_remote_copy(
+            src_ref=src, dst_ref=dst, send_sem=send, recv_sem=recv,
+            device_id=target, device_id_type=MESH,
+        )
+
+    def tile_source(position):
+        slot = core * tile_leaves + (position ^ 1)
+        return front_hbm.at[
+            pl.ds(pl.multiple_of(slot * rows, rows), rows), pl.ds(position * rows, rows)
+        ]
+
+    def each_tile(act):
+        for position in range(tile_leaves):
+            parity = (position ^ 1) % 2
+            pair = (core * tile_leaves + (position ^ 1)) // 2
+            slot = pair * 2 + parity
+            is_far = far_of(pair)
+            goal = jnp.where(is_far, 2 * row + pair % 2, slot)
+            for place, chosen in ((0, jnp.logical_not(is_far)), (1 + parity, is_far)):
+                here = at_home & chosen & (goal == col)
+                there = at_home & chosen & (goal != col)
+
+                def stay(place=place, position=position):
+                    act(
+                        pltpu.make_async_copy(
+                            tile_source(position), tile_at(place), tile_recv.at[place]
+                        ),
+                        False,
+                    )
+
+                def go(place=place, position=position, goal=goal):
+                    act(
+                        remote(
+                            tile_source(position), tile_at(place), tile_send.at[position],
+                            tile_recv.at[place], {"col": goal},
+                        ),
+                        True,
+                    )
+
+                pl.when(here)(stay)
+                pl.when(there)(go)
+
+    def start_tiles():
+        each_tile(lambda copy, away: copy.start())
+
+    def run():
+        one, two, three = (part.astype(jnp.bfloat16) for part in parts_of(work[...]))
+        both = ((1,), (1,))
+        small = fast_dot(two, two, both) + fast_dot(one, three, both) + fast_dot(three, one, both)
+        middle = fast_dot(one, two, both) + fast_dot(two, one, both)
+        wide = gram.shape[1]
+        gram[:, :probes] = fast_dot(one, one, both) + (middle + small)
+        if wide > probes:
+            gram[:, probes:] = jnp.zeros((probes, wide - probes), jnp.float32)
+
+        def near_copy(step, which):
+            span = pl.ds(pl.multiple_of(step * nb, nb), nb)
+            src, dst = ((high, near_high), (low, near_low))[which]
+            return remote(
+                src.at[span], dst.at[span], near_send.at[which, step], near_recv.at[which, step],
+                sibling,
+            )
+
+        def far_copy(step, parity):
+            span = pl.ds(pl.multiple_of(step * nb, nb), nb)
+            return remote(
+                high.at[span], far_at(parity).at[span], far_send.at[step], far_recv.at[parity, step],
+                {"col": 2 * row + chip % 2},
+            )
+
+        def slab_at(group, goal):
+            return slab.at[
+                pl.ds(pl.multiple_of(jnp.asarray(group * slab_rows, jnp.int32), 16), slab_rows),
+                pl.ds(pl.multiple_of(jnp.asarray(goal * BLOCK, jnp.int32), BLOCK), BLOCK),
+            ]
+
+        def slab_copy(group, shift, toward=1):
+            other = (col + toward * shift + col_count) % col_count
+            owner = col if toward == 1 else other
+            return remote(
+                slab_at(group, other), slab_in.at[group, owner],
+                slab_send.at[group, shift], slab_recv.at[group, shift], {"col": other},
+            )
+
+        per_slab = BLOCK // col_count
+
+        def send_slabs(group, count):
+            start = pl.multiple_of(group * BLOCK, BLOCK)
+            for block in range(per_leaf):
+                turned = exact[pl.ds(start, count), block * BLOCK : (block + 1) * BLOCK].T
+                for goal in range(col_count):
+                    place = slab_at(group, goal).at[
+                        pl.ds(block * per_slab, per_slab), pl.ds(0, count)
+                    ]
+                    place[...] = turned[
+                        goal * per_slab : (goal + 1) * per_slab
+                    ].astype(slab.dtype)
+            for shift in range(1, col_count):
+                ready = jnp.logical_not(far_of(chip) & ((col + shift) % col_count // 2 == row))
+                pl.when(ready)(lambda shift=shift: slab_copy(group, shift).start())
+            slab_in[group, col] = slab_at(group, col)[...]
+
+        def step(index, carry):
+            start = pl.multiple_of(index * nb, nb)
+            panel = gram[pl.ds(start, nb), :]
+            square = gram[pl.ds(start, nb), pl.ds(pl.multiple_of(index // 2 * 2 * nb, 2 * nb), 2 * nb)]
+            square = jnp.where(index % 2 == 0, pltpu.roll(square, nb, 1), square)
+            lane = lax.broadcasted_iota(jnp.int32, square.shape, 1)
+            eye = jnp.where(lax.broadcasted_iota(jnp.int32, square.shape, 0) == lane, 1.0, 0.0)
+            inverse = inverse_factor(jnp.where(lane >= nb, square, eye), nb)
+            inverse_parts = left_parts(inverse, 1)
+            top = fast_dot(inverse_parts, right_parts(panel), ((1,), (0,)))
+            solved = fast_dot(inverse_parts, right_parts(work[pl.ds(start, nb), :]), ((1,), (0,)))
+            scaled = solved * scale
+            rounded = scaled.astype(high.dtype)
+            exact[pl.ds(start, nb), :] = scaled
+            high[pl.ds(start, nb), :] = rounded
+            low[pl.ds(start, nb), :] = (scaled - rounded.astype(jnp.float32)).astype(low.dtype)
+            top_parts = left_parts(top[:, :probes], 0)
+            gram[...] -= fast_dot(top_parts, right_parts(top), ((0,), (0,)))
+            work[...] -= fast_dot(top_parts, right_parts(solved), ((0,), (0,)))
+
+            @pl.when(far_of(chip))
+            def _():
+                for parity in range(2):
+                    pl.when(core == parity)(lambda parity=parity: far_copy(index, parity).start())
+
+            @pl.when(jnp.logical_not(far_of(chip)))
+            def _():
+                near_copy(index, 0).start()
+                near_copy(index, 1).start()
+
+            @pl.when(index % 2 == 1)
+            def _():
+                send_slabs(index // 2, BLOCK)
+
+            return carry
+
+        lax.fori_loop(0, steps, step, 0)
+        if steps % 2 == 1:
+            send_slabs(groups - 1, nb)
+        for shift in range(1, col_count):
+
+            @pl.when(far_of(chip) & ((col + shift) % col_count // 2 == row))
+            def _(shift=shift):
+                for group in range(groups):
+                    slab_copy(group, shift).start()
+
+
+        def times(a, b):
+            return lax.dot_general(
+                a, b, (((1,), (1,)), ((), ())), preferred_element_type=jnp.float32
+            )
+
+        def core_copy(place, goal, slot):
+            return remote(
+                stage.at[place, goal], stage_in.at[slot], core_send.at[place, goal],
+                core_recv.at[slot], {"col": goal},
+            )
+
+        def send_core(place, slot, value):
+            value = (value * shrink).astype(stage.dtype)
+            for goal in range(col_count):
+                stage[place, goal, :rank_rows] = value[goal * rank_rows : (goal + 1) * rank_rows]
+
+                @pl.when(goal != col)
+                def _(goal=goal):
+                    core_copy(place, goal, slot).start()
+
+                @pl.when(goal == col)
+                def _(goal=goal):
+                    stage_in[slot] = stage[place, goal]
+
+        def wait_tile(place, source):
+            @pl.when(source == col)
+            def _():
+                pltpu.make_async_copy(
+                    front_hbm.at[pl.ds(0, rows), pl.ds(0, rows)], tile_at(place),
+                    tile_recv.at[place],
+                ).wait()
+
+            @pl.when(source != col)
+            def _():
+                remote(
+                    front_hbm.at[pl.ds(0, rows), pl.ds(0, rows)], tile_at(place), tile_send.at[0],
+                    tile_recv.at[place], {"col": source},
+                ).wait_recv()
+
+        @pl.when(jnp.logical_not(far_of(chip)))
+        def _():
+            wait_tile(0, 2 * row + col // tile_leaves)
+            for index in range(steps):
+                near_copy(index, 0).wait_recv()
+                near_copy(index, 1).wait_recv()
+            product = (times(near_high[...], tile_at(0)[...]) + times(near_low[...], tile_at(0)[...])) * shrink
+            rounded = product.astype(jnp.bfloat16)
+            rest = (product - rounded.astype(jnp.float32)).astype(jnp.bfloat16)
+            send_core(
+                0, col,
+                times(high[...], rounded) + (times(low[...], rounded) + times(high[...], rest)),
+            )
+
+        for pair in range(chips):
+
+            @pl.when(at_home & far_of(pair) & (core == pair % 2))
+            def _(pair=pair):
+                for parity in range(2):
+                    for index in range(steps):
+                        span = pl.ds(index * nb, nb)
+                        remote(
+                            high.at[span], far_at(parity).at[span], far_send.at[index],
+                            far_recv.at[parity, index], {"col": 2 * pair + parity},
+                        ).wait_recv()
+                for parity in range(2):
+                    slot = 2 * pair + parity
+                    wait_tile(1 + parity, 2 * row + slot // tile_leaves)
+                    product = times(far_at(1 - parity)[...], tile_at(1 + parity)[...]) * shrink
+                    send_core(1 + parity, slot, times(far_at(parity)[...], product.astype(jnp.bfloat16)))
+
+        for group in range(groups):
+            for shift in range(1, col_count):
+                slab_copy(group, shift, -1).wait_recv()
+        for slot in range(col_count):
+            for group in range(groups):
+                count = min(BLOCK, probes - group * BLOCK)
+                basis_ref[
+                    slot * per_leaf : (slot + 1) * per_leaf, :, group * BLOCK : group * BLOCK + count
+                ] = slab_in[group, slot].reshape(per_leaf, per_slab, BLOCK)[:, :, :count]
+        for slot in range(col_count):
+            pair = slot // 2
+            source = jnp.where(far_of(pair), 2 * row + pair % 2, slot)
+
+            @pl.when(source != col)
+            def _(slot=slot, source=source):
+                remote(
+                    stage.at[0, 0], stage_in.at[slot], core_send.at[0, 0], core_recv.at[slot],
+                    {"col": source},
+                ).wait_recv()
+
+            core_ref[slot] = stage_in[slot, :rank_rows].astype(jnp.float32)
+
+        def settle(copy, away):
+            if away:
+                copy.wait_send()
+
+        each_tile(settle)
+
+        @pl.when(far_of(chip))
+        def _():
+            for index in range(steps):
+                far_copy(index, 0).wait_send()
+
+        @pl.when(jnp.logical_not(far_of(chip)))
+        def _():
+            for index in range(steps):
+                near_copy(index, 0).wait_send()
+                near_copy(index, 1).wait_send()
+            for goal in range(col_count):
+                pl.when(goal != col)(lambda goal=goal: core_copy(0, goal, col).wait_send())
+
+        for group in range(groups):
+            for shift in range(1, col_count):
+                slab_copy(group, shift).wait_send()
+        for pair in range(chips):
+
+            @pl.when(at_home & far_of(pair) & (core == pair % 2))
+            def _(pair=pair):
+                for parity in range(2):
+                    for goal in range(col_count):
+                        pl.when(goal != col)(
+                            lambda goal=goal, parity=parity: core_copy(
+                                1 + parity, goal, 2 * pair + parity
+                            ).wait_send()
+                        )
+
+    return start_tiles, run
+
+
 def spread(total, parts, grain):
     base = total // grain
     cuts = [base * (i + 1) // parts * grain for i in range(parts)]
@@ -178,7 +507,8 @@
     test_hbm,
     kids_hbm,
     front_hbm,
-    yt_ref,
+    basis_ref,
+    core_ref,
     kid_test,
     test,
     ring,
@@ -190,8 +520,6 @@
     came,
     came_two,
     kids,
-    merged,
-    landed,
     load_sem,
     test_sem,
     swap_send,
@@ -206,13 +534,19 @@
     row_recv,
     leaf_send,
     leaf_recv,
+    slab_in,
+    stage_out,
+    stage_in,
+    ready,
+    *sems,
 ):
     row_count, col_count, kid_tiles, kid_each, order, slots, subs = dims
     chips = col_count // 2
-    probes, rows = yt_ref.shape
+    probes, rows = parts.shape[1:]
     half = probes // 2
     per_leaf = rows // BLOCK
-    blocks = merged.shape[0]
+    blocks = front_hbm.shape[0] // BLOCK
+    most = kids.shape[1]
     pieces = slots
     row, col = lax.axis_index("row"), lax.axis_index("col")
     chip, core = col // 2, col % 2
@@ -529,6 +863,12 @@
 
     lax.fori_loop(0, turns, turn_of, 0)
     combine(chips - 1)
+    for at in range(chips - 2, chips):
+        swap(at).wait_send()
+    for shift in range(1, col_count):
+        pl.semaphore_signal(
+            ready, inc=1, device_id={"col": (col + shift) % col_count}, device_id_type=MESH
+        )
     if order[-1] > 0:
         head(order[-1], 0)
     for pair in (order[-1], order[-2]):
@@ -547,12 +887,16 @@
     chain(order[:2])
     chain(order[2:])
 
+    landing = pl.ds(2 * rows, rows)
+    leaving = 3 * rows
+
     def leaf_move(shift, here):
-        size = pieces[here][1]
+        start, size = pieces[here]
         goal = (col + shift) % col_count
+        src = pl.ds(pl.multiple_of(goal * most, most), size)
+        dst = pl.ds(pl.multiple_of(core * half + start, 16), size)
         return remote(
-            merged.at[pl.ds(goal * per_leaf, per_leaf), pl.ds(0, size)],
-            landed.at[col, :, pl.ds(0, size)],
+            ring.at[1, src, pl.ds(leaving, rows)], ring.at[1, dst, landing],
             leaf_send.at[shift - 1], leaf_recv.at[shift - 1], {"col": goal},
         )
 
@@ -569,15 +913,45 @@
         def one(block, carry):
             first = kids[picks_ref[0, block], :size]
             second = kids[picks_ref[1, block], :size]
-            merged[block, :size] = (first + second).astype(jnp.bfloat16)
+            goal = block // per_leaf
+            lane = pl.multiple_of(leaving + block % per_leaf * BLOCK, BLOCK)
+            ring[1, pl.ds(pl.multiple_of(goal * most, most), size), pl.ds(lane, BLOCK)] = (
+                first + second
+            ).astype(jnp.bfloat16)
             return carry
 
         lax.fori_loop(0, blocks, one, 0)
         for shift in range(1, col_count):
             leaf_move(shift, here).start()
-        landed[col, :, :size] = merged[pl.ds(col * per_leaf, per_leaf), :size]
-
+        start = pieces[here][0]
+        dst = pl.ds(pl.multiple_of(core * half + start, 16), size)
+        src = pl.ds(pl.multiple_of(col * most, most), size)
+        ring[1, dst, landing] = ring[1, src, pl.ds(leaving, rows)]
+
+    pl.semaphore_wait(ready, col_count - 1)
     each_chip(merge)
+    work = parts.at[1]
+    start_tiles, run = finishing(
+        (row_count, col_count, test.shape[1] // rows),
+        lambda place: ring.at[0, :, pl.ds(place * rows, rows)],
+        lambda parity: ring.at[1, pl.ds(parity * probes, probes), pl.ds(0, rows)],
+        front_hbm,
+        basis_ref,
+        core_ref,
+        parts.at[3, :, pl.ds(0, slab_in.shape[0] * BLOCK)],
+        work,
+        parts.at[0],
+        ring.at[1, pl.ds(0, probes), pl.ds(rows, rows)],
+        ring.at[1, pl.ds(probes, probes), pl.ds(rows, rows)],
+        ring.at[0, pl.ds(0, probes), pl.ds(3 * rows, rows)],
+        ring.at[0, pl.ds(probes, probes), pl.ds(3 * rows, rows)],
+        test,
+        slab_in,
+        stage_out,
+        stage_in,
+        sems,
+    )
+    start_tiles()
 
     def land():
         for shift in range(1, col_count):
@@ -586,25 +960,18 @@
             for there in range(chips):
 
                 def wait(there=there):
-                    size = pieces[there][1]
+                    start, size = pieces[there]
+                    dst = pl.ds(pl.multiple_of(source % 2 * half + start, 16), size)
                     remote(
-                        merged.at[pl.ds(0, per_leaf), pl.ds(0, size)],
-                        landed.at[source, :, pl.ds(0, size)],
+                        ring.at[1, pl.ds(0, size), pl.ds(leaving, rows)],
+                        ring.at[1, dst, landing],
                         leaf_send.at[shift - 1], leaf_recv.at[shift - 1], {"col": source},
                     ).wait_recv()
 
                 pl.when(far == there)(wait)
 
     land()
-    for source in range(col_count):
-        start, size = pieces[source // 2]
-        start += source % 2 * half
-        for block in range(per_leaf):
-            lanes = pl.ds(block * BLOCK, BLOCK)
-            yt_ref[pl.ds(start, size), lanes] = (
-                sums[chip, pl.ds(start, size), lanes]
-                + landed[source, block, :size].astype(jnp.float32)
-            )
+    work[...] = sums[chip] + ring[1, :probes, 2 * rows : 3 * rows].astype(jnp.float32)
 
     def drain(here):
         def one(tile, carry):
@@ -623,9 +990,8 @@
         for shift in range(1, col_count):
             leaf_move(shift, here).wait_send()
 
+    run()
     each_chip(drain)
-    for at in range(chips - 2, chips):
-        swap(at).wait_send()
 
 
 def sample_of(picks, kid_test, test, kids, front, row_count, col_count):
@@ -646,14 +1012,25 @@
         order += [high] if low == high else [high, low]
         low, high = low + 1, high - 1
     f32, bf16 = jnp.float32, jnp.bfloat16
+    steps = probes // PIVOTS
+    groups = -(-probes // BLOCK)
+    rank_rows = probes // col_count
+    padded = -(-rank_rows // 16) * 16
+    slab = pltpu.VMEM((groups, col_count, per_leaf * (BLOCK // col_count), BLOCK), bf16)
     dims = (row_count, col_count, kid_tiles, kid_each, tuple(order), tuple(pieces), subs)
     any_spec = pl.BlockSpec(memory_space=pl.ANY)
     dma = pltpu.SemaphoreType.DMA
     return pl.pallas_call(
         functools.partial(sample_kernel, dims),
-        out_shape=jax.ShapeDtypeStruct((probes, LEAF), f32),
+        out_shape=(
+            jax.ShapeDtypeStruct((blocks, BLOCK // col_count, probes), bf16),
+            jax.ShapeDtypeStruct((col_count, rank_rows, probes), f32),
+        ),
         in_specs=[pl.BlockSpec(memory_space=pltpu.SMEM)] + [any_spec] * 4,
-        out_specs=pl.BlockSpec(memory_space=pltpu.VMEM),
+        out_specs=(
+            pl.BlockSpec(memory_space=pltpu.VMEM),
+            pl.BlockSpec(memory_space=pltpu.VMEM),
+        ),
         scratch_shapes=[
             pltpu.VMEM((kids.shape[0], probes, kid_depth), bf16),
             pltpu.VMEM((probes, depth), bf16),
@@ -666,8 +1043,6 @@
             pltpu.VMEM((chips, probes, LEAF), bf16),
             pltpu.VMEM((probes, LEAF), bf16),
             pltpu.VMEM((row_count * blocks + 1, most, BLOCK), f32),
-            pltpu.VMEM((blocks, most, BLOCK), bf16),
-            pltpu.VMEM((col_count, per_leaf, most, BLOCK), bf16),
             dma((2,)),
             dma((2,)),
             dma((kid_tiles + chips,)),
@@ -682,6 +1057,20 @@
             dma((kid_tiles, row_count - 1)),
             dma((col_count - 1,)),
             dma((col_count - 1,)),
+            slab,
+            pltpu.VMEM((3, col_count, padded, probes), bf16),
+            pltpu.VMEM((col_count, padded, probes), bf16),
+            pltpu.SemaphoreType.REGULAR,
+            dma((depth // LEAF,)),
+            dma((3,)),
+            dma((2, steps)),
+            dma((2, steps)),
+            dma((steps,)),
+            dma((2, steps)),
+            dma((groups, col_count)),
+            dma((groups, col_count)),
+            dma((3, col_count)),
+            dma((col_count,)),
         ],
         compiler_params=pltpu.CompilerParams(
             collective_id=0, has_side_effects=True, vmem_limit_bytes=67043328
@@ -693,379 +1082,6 @@
         ),
         name="sample",
     )(picks, kid_test, test, kids, front)
-
-
-def finish_kernel(
-    dims,
-    yt_ref,
-    front_hbm,
-    basis_ref,
-    core_ref,
-    gram,
-    work,
-    exact,
-    high,
-    low,
-    near_high,
-    near_low,
-    far,
-    tile,
-    slab,
-    slab_in,
-    stage,
-    stage_in,
-    tile_send,
-    tile_recv,
-    near_send,
-    near_recv,
-    far_send,
-    far_recv,
-    slab_send,
-    slab_recv,
-    core_send,
-    core_recv,
-):
-    _, col_count, tile_leaves = dims
-    nb = PIVOTS
-    chips = col_count // 2
-    probes, rows = yt_ref.shape
-    per_leaf = rows // BLOCK
-    rank_rows = probes // col_count
-    groups = slab.shape[0]
-    steps = probes // nb
-    scale = math.sqrt(LEAF)
-    shrink = 1.0 / scale
-    row, col = lax.axis_index("row"), lax.axis_index("col")
-    chip, core = col // 2, col % 2
-    sibling = {"col": chip * 2 + 1 - core}
-    at_home = chip == row
-
-    def far_of(pair):
-        return (pair >= row + 2) | (pair + 2 <= row)
-
-    def remote(src, dst, send, recv, target):
-        return pltpu.make_async_remote_copy(
-            src_ref=src, dst_ref=dst, send_sem=send, recv_sem=recv,
-            device_id=target, device_id_type=MESH,
-        )
-
-    barrier = pltpu.get_barrier_semaphore()
-    for shift in range(1, col_count):
-        pl.semaphore_signal(
-            barrier, inc=1, device_id={"col": (col + shift) % col_count}, device_id_type=MESH
-        )
-    pl.semaphore_wait(barrier, col_count - 1)
-
-    def tile_source(position):
-        slot = core * tile_leaves + (position ^ 1)
-        return front_hbm.at[
-            pl.ds(pl.multiple_of(slot * rows, rows), rows), pl.ds(position * rows, rows)
-        ]
-
-    def each_tile(act):
-        for position in range(tile_leaves):
-            parity = (position ^ 1) % 2
-            pair = (core * tile_leaves + (position ^ 1)) // 2
-            slot = pair * 2 + parity
-            is_far = far_of(pair)
-            goal = jnp.where(is_far, 2 * row + pair % 2, slot)
-            for place, chosen in ((0, jnp.logical_not(is_far)), (1 + parity, is_far)):
-                here = at_home & chosen & (goal == col)
-                there = at_home & chosen & (goal != col)
-
-                def stay(place=place, position=position):
-                    act(
-                        pltpu.make_async_copy(
-                            tile_source(position), tile.at[place], tile_recv.at[place]
-                        ),
-                        False,
-                    )
-
-                def go(place=place, position=position, goal=goal):
-                    act(
-                        remote(
-                            tile_source(position), tile.at[place], tile_send.at[position],
-                            tile_recv.at[place], {"col": goal},
-                        ),
-                        True,
-                    )
-
-                pl.when(here)(stay)
-                pl.when(there)(go)
-
-    each_tile(lambda copy, away: copy.start())
-
-    work[...] = yt_ref[...]
-    gram[...] = dot(yt_ref[...], yt_ref[...], ((1,), (1,)))
-
-    def near_copy(step, which):
-        span = pl.ds(pl.multiple_of(step * nb, nb), nb)
-        src, dst = ((high, near_high), (low, near_low))[which]
-        return remote(
-            src.at[span], dst.at[span], near_send.at[which, step], near_recv.at[which, step],
-            sibling,
-        )
-
-    def far_copy(step, parity):
-        span = pl.ds(pl.multiple_of(step * nb, nb), nb)
-        return remote(
-            high.at[span], far.at[parity, span], far_send.at[step], far_recv.at[parity, step],
-            {"col": 2 * row + chip % 2},
-        )
-
-    def slab_copy(group, shift, toward=1):
-        other = (col + toward * shift + col_count) % col_count
-        owner = col if toward == 1 else other
-        return remote(
-            slab.at[group, other], slab_in.at[group, owner],
-            slab_send.at[group, shift], slab_recv.at[group, shift], {"col": other},
-        )
-
-    per_slab = BLOCK // col_count
-
-    def send_slabs(group, count):
-        start = pl.multiple_of(group * BLOCK, BLOCK)
-        for block in range(per_leaf):
-            turned = exact[pl.ds(start, count), block * BLOCK : (block + 1) * BLOCK].T
-            for goal in range(col_count):
-                slab[group, goal, block, :, :count] = turned[
-                    goal * per_slab : (goal + 1) * per_slab
-                ].astype(slab.dtype)
-        for shift in range(1, col_count):
-            slab_copy(group, shift).start()
-        slab_in[group, col] = slab[group, col]
-
-    def step(index, carry):
-        start = pl.multiple_of(index * nb, nb)
-        panel = gram[pl.ds(start, nb), :]
-        source = lax.broadcasted_iota(jnp.int32, (probes, 2 * nb), 0)
-        lane = lax.broadcasted_iota(jnp.int32, (probes, 2 * nb), 1)
-        pick = jnp.where((lane >= nb) & (source == lane - nb + start), 1.0, 0.0)
-        eye = jnp.where(
-            lax.broadcasted_iota(jnp.int32, (nb, 2 * nb), 0)
-            == lax.broadcasted_iota(jnp.int32, (nb, 2 * nb), 1),
-            1.0,
-            0.0,
-        )
-        inverse = inverse_factor(dot(panel, pick, ((1,), (0,))) + eye, nb)
-        top = dot(inverse, panel, ((1,), (0,)))
-        solved = dot(inverse, work[pl.ds(start, nb), :], ((1,), (0,)))
-        scaled = solved * scale
-        rounded = scaled.astype(high.dtype)
-        exact[pl.ds(start, nb), :] = scaled
-        high[pl.ds(start, nb), :] = rounded
-        low[pl.ds(start, nb), :] = (scaled - rounded.astype(jnp.float32)).astype(low.dtype)
-        gram[...] -= dot(top, top, ((0,), (0,)))
-        work[...] -= dot(top, solved, ((0,), (0,)))
-
-        @pl.when(far_of(chip))
-        def _():
-            for parity in range(2):
-                pl.when(core == parity)(lambda parity=parity: far_copy(index, parity).start())
-
-        @pl.when(jnp.logical_not(far_of(chip)))
-        def _():
-            near_copy(index, 0).start()
-            near_copy(index, 1).start()
-
-        @pl.when(index % 2 == 1)
-        def _():
-            send_slabs(index // 2, BLOCK)
-
-        return carry
-
-    lax.fori_loop(0, steps, step, 0)
-    if steps % 2 == 1:
-        send_slabs(groups - 1, nb)
-
-    def times(a, b):
-        return lax.dot_general(
-            a, b, (((1,), (1,)), ((), ())), preferred_element_type=jnp.float32
-        )
-
-    def core_copy(place, goal, slot):
-        return remote(
-            stage.at[place, goal], stage_in.at[slot], core_send.at[place, goal],
-            core_recv.at[slot], {"col": goal},
-        )
-
-    def send_core(place, slot, value):
-        value = (value * shrink).astype(stage.dtype)
-        for goal in range(col_count):
-            stage[place, goal, :rank_rows] = value[goal * rank_rows : (goal + 1) * rank_rows]
-
-            @pl.when(goal != col)
-            def _(goal=goal):
-                core_copy(place, goal, slot).start()
-
-            @pl.when(goal == col)
-            def _(goal=goal):
-                stage_in[slot] = stage[place, goal]
-
-    def wait_tile(place, source):
-        @pl.when(source == col)
-        def _():
-            pltpu.make_async_copy(
-                front_hbm.at[pl.ds(0, rows), pl.ds(0, rows)], tile.at[place],
-                tile_recv.at[place],
-            ).wait()
-
-        @pl.when(source != col)
-        def _():
-            remote(
-                front_hbm.at[pl.ds(0, rows), pl.ds(0, rows)], tile.at[place], tile_send.at[0],
-                tile_recv.at[place], {"col": source},
-            ).wait_recv()
-
-    @pl.when(jnp.logical_not(far_of(chip)))
-    def _():
-        wait_tile(0, 2 * row + col // tile_leaves)
-        for index in range(steps):
-            near_copy(index, 0).wait_recv()
-            near_copy(index, 1).wait_recv()
-        product = (times(near_high[...], tile[0]) + times(near_low[...], tile[0])) * shrink
-        rounded = product.astype(jnp.bfloat16)
-        rest = (product - rounded.astype(jnp.float32)).astype(jnp.bfloat16)
-        send_core(
-            0, col,
-            times(high[...], rounded) + (times(low[...], rounded) + times(high[...], rest)),
-        )
-
-    for pair in range(chips):
-
-        @pl.when(at_home & far_of(pair) & (core == pair % 2))
-        def _(pair=pair):
-            for parity in range(2):
-                for index in range(steps):
-                    span = pl.ds(index * nb, nb)
-                    remote(
-                        high.at[span], far.at[parity, span], far_send.at[index],
-                        far_recv.at[parity, index], {"col": 2 * pair + parity},
-                    ).wait_recv()
-            for parity in range(2):
-                slot = 2 * pair + parity
-                wait_tile(1 + parity, 2 * row + slot // tile_leaves)
-                product = times(far[1 - parity], tile[1 + parity]) * shrink
-                send_core(1 + parity, slot, times(far[parity], product.astype(jnp.bfloat16)))
-
-    for group in range(groups):
-        for shift in range(1, col_count):
-            slab_copy(group, shift, -1).wait_recv()
-    for slot in range(col_count):
-        for group in range(groups):
-            count = min(BLOCK, probes - group * BLOCK)
-            basis_ref[
-                slot * per_leaf : (slot + 1) * per_leaf, :, group * BLOCK : group * BLOCK + count
-            ] = slab_in[group, slot, :, :, :count]
-    for slot in range(col_count):
-        pair = slot // 2
-        source = jnp.where(far_of(pair), 2 * row + pair % 2, slot)
-
-        @pl.when(source != col)
-        def _(slot=slot, source=source):
-            remote(
-                stage.at[0, 0], stage_in.at[slot], core_send.at[0, 0], core_recv.at[slot],
-                {"col": source},
-            ).wait_recv()
-
-        core_ref[slot] = stage_in[slot, :rank_rows].astype(jnp.float32)
-
-    def settle(copy, away):
-        if away:
-            copy.wait_send()
-
-    each_tile(settle)
-
-    @pl.when(far_of(chip))
-    def _():
-        for index in range(steps):
-            far_copy(index, 0).wait_send()
-
-    @pl.when(jnp.logical_not(far_of(chip)))
-    def _():
-        for index in range(steps):
-            near_copy(index, 0).wait_send()
-            near_copy(index, 1).wait_send()
-        for goal in range(col_count):
-            pl.when(goal != col)(lambda goal=goal: core_copy(0, goal, col).wait_send())
-
-    for group in range(groups):
-        for shift in range(1, col_count):
-            slab_copy(group, shift).wait_send()
-    for pair in range(chips):
-
-        @pl.when(at_home & far_of(pair) & (core == pair % 2))
-        def _(pair=pair):
-            for parity in range(2):
-                for goal in range(col_count):
-                    pl.when(goal != col)(
-                        lambda goal=goal, parity=parity: core_copy(
-                            1 + parity, goal, 2 * pair + parity
-                        ).wait_send()
-                    )
-
-
-def finish(yt, front, row_count, col_count):
-    probes, rows = yt.shape
-    steps = probes // PIVOTS
-    per_leaf = rows // BLOCK
-    blocks = front.shape[0] // BLOCK
-    groups = -(-probes // BLOCK)
-    rank_rows = probes // col_count
-    padded = -(-rank_rows // 16) * 16
-    f32, bf16 = jnp.float32, jnp.bfloat16
-    dma = pltpu.SemaphoreType.DMA
-    slab = pltpu.VMEM((groups, col_count, per_leaf, BLOCK // col_count, BLOCK), bf16)
-    dims = (row_count, col_count, front.shape[1] // LEAF)
-    return pl.pallas_call(
-        functools.partial(finish_kernel, dims),
-        out_shape=(
-            jax.ShapeDtypeStruct((blocks, BLOCK // col_count, probes), bf16),
-            jax.ShapeDtypeStruct((col_count, rank_rows, probes), f32),
-        ),
-        in_specs=[
-            pl.BlockSpec(memory_space=pltpu.VMEM),
-            pl.BlockSpec(memory_space=pl.ANY),
-        ],
-        out_specs=(
-            pl.BlockSpec(memory_space=pltpu.VMEM),
-            pl.BlockSpec(memory_space=pltpu.VMEM),
-        ),
-        scratch_shapes=[
-            pltpu.VMEM((probes, probes), f32),
-            pltpu.VMEM((probes, rows), f32),
-            pltpu.VMEM((probes, rows), f32),
-            pltpu.VMEM((probes, rows), bf16),
-            pltpu.VMEM((probes, rows), bf16),
-            pltpu.VMEM((probes, rows), bf16),
-            pltpu.VMEM((probes, rows), bf16),
-            pltpu.VMEM((2, probes, rows), bf16),
-            pltpu.VMEM((3, rows, rows), bf16),
-            slab,
-            slab,
-            pltpu.VMEM((3, col_count, padded, probes), bf16),
-            pltpu.VMEM((col_count, padded, probes), bf16),
-            dma((dims[2],)),
-            dma((3,)),
-            dma((2, steps)),
-            dma((2, steps)),
-            dma((steps,)),
-            dma((2, steps)),
-            dma((groups, col_count)),
-            dma((groups, col_count)),
-            dma((3, col_count)),
-            dma((col_count,)),
-        ],
-        compiler_params=pltpu.CompilerParams(
-            collective_id=1, has_side_effects=True, vmem_limit_bytes=56 << 20
-        ),
-        cost_estimate=pl.CostEstimate(
-            flops=40 * probes * probes * rows,
-            bytes_accessed=6 * probes * rows,
-            transcendentals=0,
-        ),
-        name="finish",
-    )(yt, front)
 
 
 def general(parent_front, child_update, parent_test, child_test, child_map):
@@ -1169,7 +1185,7 @@
     return (leaf_basis, cores[:leaf_count])
 
 
-def fits(parent_front, child_update, row_count, col_count):
+def fits(parent_front, child_update, parent_test, row_count, col_count):
     leaf_count = parent_front.shape[0] // LEAF
     return (
         leaf_count == col_count
@@ -1183,6 +1199,10 @@
         and parent_front.shape[1] // LEAF * 2 == leaf_count
         and col_count % 2 == 0
         and parent_front.shape[1] % LEAF == 0
+        and 2 * PIVOTS == BLOCK
+        and parent_front.shape[1] >= 4 * LEAF
+        and LEAF // col_count * -(-parent_test.shape[1] // BLOCK) <= parent_test.shape[1]
+        and parent_test.shape[1] * 2 <= LEAF
         and child_update.shape[1] % LEAF == 0
         and 2 * parent_front.shape[1] * LEAF * 2 < 16 << 20
     )
@@ -1203,16 +1223,16 @@
 def local(parent_front, child_update, parent_test, child_test, child_map):
     row_count = lax.axis_size("row")
     col_count = lax.axis_size("col")
-    if not fits(parent_front, child_update, row_count, col_count):
+    if not fits(parent_front, child_update, parent_test, row_count, col_count):
         return general(parent_front, child_update, parent_test, child_test, child_map)
     row_index = lax.axis_index("row")
     own_blocks = parent_front.shape[0] // BLOCK
     picks = picks_of(child_map, row_index, row_count, own_blocks)
-    yt = sample_of(
+    outs = sample_of(
         picks, child_test.transpose(0, 2, 1), parent_test.T, child_update, parent_front,
         row_count, col_count,
     )
-    return tuple(finish(yt, parent_front, row_count, col_count))
+    return tuple(outs)
 
 
 def solution(mesh):

time: 227 us -> 217 us (0.956)
  the two profiles are of different devices: /device:TPU:0 before, /device:TPU:27 now
where the time goes in v2:
time: 217 us; the launch traced here: 216 us
  Pallas kernels  210 us (97%)
  local copies, waits for them, and re-layouts  4.32 us (2%)
    pallas_call x1, Pallas kernels, sample_of(): pl.pallas_call(functools.partial(sample_kernel, dims), out_shape=(jax.Sha...  210 us

profile of v2, /device:TPU:27, one launch (start us, length us, event | category | flops | bytes accessed | tf_op | source)
XLA Modules:
  0.0 216.5 jit_solution(8935890689238808274)
XLA Ops:
  0.7 0.8 broadcast_add_fusion
  1.4 0.1 select_reduce_fusion
  1.5 0.6 compare_select_fusion.picks_ref
  2.1 210.0 %sample.1 = (bf16[56,16,448]{2,1,0:T(8,128)(2,1)}, f32[8,56,448]{2,1,0:T(8,128)}) custom-call(s32[2,56]{1,0:T(2,128)} %compare_select_fusion.picks_ref, bf16[2,448,1792]{2,1,0:T(8,128)(2,1)} %bitcast.2, bf16[448,3584]{1,0:T(8,128)(2,1)} %bitcast.3, bf16[2,3584,1792]{2,1,0:T(8,128)(2,1)} %kids_hbm.1, bf16[7168,3584]{1,0:T(8,128)(2,1)} %front_hbm.1), custom_call_target="tpu_custom_call" | custom-call | flops 46036680704 | bytes 102760448 | tf_op jit(solution)/shard_map/sample/pallas_call | solution.py:1023
  212.1 2.2 copy.9
  214.3 2.2 copy.10
  (2 shorter events, 0.0 us)

commit v3 on v2

--- a/solution.py
+++ b/solution.py
@@ -203,6 +203,9 @@
     probes, rows = work.shape
     per_leaf = rows // BLOCK
     rank_rows = probes // col_count
+    whole = probes // BLOCK * BLOCK
+    fold = -(-rank_rows // 16) * 8
+    packed = stage_in.shape[1]
     steps = probes // nb
     scale = math.sqrt(LEAF)
     shrink = 1.0 / scale
@@ -356,13 +359,6 @@
         lax.fori_loop(0, steps, step, 0)
         if steps % 2 == 1:
             send_slabs(groups - 1, nb)
-        for shift in range(1, col_count):
-
-            @pl.when(far_of(chip) & ((col + shift) % col_count // 2 == row))
-            def _(shift=shift):
-                for group in range(groups):
-                    slab_copy(group, shift).start()
-
 
         def times(a, b):
             return lax.dot_general(
@@ -376,9 +372,17 @@
             )
 
         def send_core(place, slot, value):
-            value = (value * shrink).astype(stage.dtype)
+            value = value * shrink
             for goal in range(col_count):
-                stage[place, goal, :rank_rows] = value[goal * rank_rows : (goal + 1) * rank_rows]
+                piece = value[goal * rank_rows : (goal + 1) * rank_rows]
+                columns = [piece[:, at : at + BLOCK] for at in range(0, whole, BLOCK)]
+                last = jnp.concatenate(
+                    [piece[:fold, whole:], piece[rank_rows - fold :, whole:]], axis=1
+                )
+                filler = jnp.zeros((packed - len(columns) * rank_rows - fold, BLOCK), jnp.float32)
+                stage[place, goal] = jnp.concatenate(columns + [last, filler], axis=0).astype(
+                    stage.dtype
+                )
 
                 @pl.when(goal != col)
                 def _(goal=goal):
@@ -434,9 +438,31 @@
                     product = times(far_at(1 - parity)[...], tile_at(1 + parity)[...]) * shrink
                     send_core(1 + parity, slot, times(far_at(parity)[...], product.astype(jnp.bfloat16)))
 
-        for group in range(groups):
-            for shift in range(1, col_count):
-                slab_copy(group, shift, -1).wait_recv()
+        def late(shift):
+            other = (col - shift + col_count) % col_count
+            return at_home & far_of(other // 2)
+
+        for shift in range(1, col_count):
+
+            @pl.when(jnp.logical_not(late(shift)))
+            def _(shift=shift):
+                for group in range(groups):
+                    slab_copy(group, shift, -1).wait_recv()
+
+        for shift in range(1, col_count):
+
+            @pl.when(far_of(chip) & ((col + shift) % col_count // 2 == row))
+            def _(shift=shift):
+                for group in range(groups):
+                    slab_copy(group, shift).start()
+
+        for shift in range(1, col_count):
+
+            @pl.when(late(shift))
+            def _(shift=shift):
+                for group in range(groups):
+                    slab_copy(group, shift, -1).wait_recv()
+
         for slot in range(col_count):
             for group in range(groups):
                 count = min(BLOCK, probes - group * BLOCK)
@@ -454,7 +480,13 @@
                     {"col": source},
                 ).wait_recv()
 
-            core_ref[slot] = stage_in[slot, :rank_rows].astype(jnp.float32)
+            came = stage_in[slot].astype(jnp.float32)
+            for at in range(0, whole, BLOCK):
+                first = at // BLOCK * rank_rows
+                core_ref[slot, :, at : at + BLOCK] = came[first : first + rank_rows]
+            last = came[whole // BLOCK * rank_rows :][:fold]
+            core_ref[slot, :fold, whole:] = last[:, : probes - whole]
+            core_ref[slot, fold:, whole:] = last[2 * fold - rank_rows :, probes - whole :]
 
         def settle(copy, away):
             if away:
@@ -705,7 +737,7 @@
             for block in range(per_leaf):
                 kids[row * blocks + tile * per_leaf + block, :size] = kid_sum[
                     tile, start : start + size, block * BLOCK : (block + 1) * BLOCK
-                ]
+                ].astype(kids.dtype)
             for shift in range(1, row_count):
                 kid_share(tile, shift, here).start()
 
@@ -885,7 +917,6 @@
 
     lax.fori_loop(turns, kid_tiles + chips - 2, tail_turn, 0)
     chain(order[:2])
-    chain(order[2:])
 
     landing = pl.ds(2 * rows, rows)
     leaving = 3 * rows
@@ -911,8 +942,8 @@
         lax.fori_loop(0, kid_tiles, arrive, 0)
 
         def one(block, carry):
-            first = kids[picks_ref[0, block], :size]
-            second = kids[picks_ref[1, block], :size]
+            first = kids[picks_ref[0, block], :size].astype(jnp.float32)
+            second = kids[picks_ref[1, block], :size].astype(jnp.float32)
             goal = block // per_leaf
             lane = pl.multiple_of(leaving + block % per_leaf * BLOCK, BLOCK)
             ring[1, pl.ds(pl.multiple_of(goal * most, most), size), pl.ds(lane, BLOCK)] = (
@@ -930,6 +961,7 @@
 
     pl.semaphore_wait(ready, col_count - 1)
     each_chip(merge)
+    chain(order[2:])
     work = parts.at[1]
     start_tiles, run = finishing(
         (row_count, col_count, test.shape[1] // rows),
@@ -1015,7 +1047,8 @@
     steps = probes // PIVOTS
     groups = -(-probes // BLOCK)
     rank_rows = probes // col_count
-    padded = -(-rank_rows // 16) * 16
+    packed = probes // BLOCK * rank_rows + -(-rank_rows // 16) * 8
+    packed = -(-packed // 16) * 16
     slab = pltpu.VMEM((groups, col_count, per_leaf * (BLOCK // col_count), BLOCK), bf16)
     dims = (row_count, col_count, kid_tiles, kid_each, tuple(order), tuple(pieces), subs)
     any_spec = pl.BlockSpec(memory_space=pl.ANY)
@@ -1042,7 +1075,7 @@
             pltpu.VMEM((kid_tiles, most, LEAF), bf16),
             pltpu.VMEM((chips, probes, LEAF), bf16),
             pltpu.VMEM((probes, LEAF), bf16),
-            pltpu.VMEM((row_count * blocks + 1, most, BLOCK), f32),
+            pltpu.VMEM((row_count * blocks + 1, most, BLOCK), bf16),
             dma((2,)),
             dma((2,)),
             dma((kid_tiles + chips,)),
@@ -1058,8 +1091,8 @@
             dma((col_count - 1,)),
             dma((col_count - 1,)),
             slab,
-            pltpu.VMEM((3, col_count, padded, probes), bf16),
-            pltpu.VMEM((col_count, padded, probes), bf16),
+            pltpu.VMEM((3, col_count, packed, BLOCK), bf16),
+            pltpu.VMEM((col_count, packed, BLOCK), bf16),
             pltpu.SemaphoreType.REGULAR,
             dma((depth // LEAF,)),
             dma((3,)),
@@ -1203,6 +1236,8 @@
         and parent_front.shape[1] >= 4 * LEAF
         and LEAF // col_count * -(-parent_test.shape[1] // BLOCK) <= parent_test.shape[1]
         and parent_test.shape[1] * 2 <= LEAF
+        and parent_test.shape[1] % BLOCK * 2 == BLOCK
+        and parent_test.shape[1] % (8 * col_count) == 0
         and child_update.shape[1] % LEAF == 0
         and 2 * parent_front.shape[1] * LEAF * 2 < 16 << 20
     )

time: 217 us -> 210 us (0.968)
  the two profiles are of different devices: /device:TPU:27 before, /device:TPU:0 now
where the time goes in v3:
time: 210 us; the launch traced here: 208 us
  Pallas kernels  202 us (96%)
  local copies, waits for them, and re-layouts  4.32 us (2%)
    pallas_call x1, Pallas kernels, sample_of(): pl.pallas_call(functools.partial(sample_kernel, dims), out_shape=(jax.Sha...  202 us
    unnamed x2, local copies, waits for them, and re-layouts  4.32 us

profile of v3, /device:TPU:0, one launch (start us, length us, event | category | flops | bytes accessed | tf_op | source)
XLA Modules:
  0.0 208.3 jit_solution(8806398422368579165)
XLA Ops:
  0.7 0.8 broadcast_add_fusion
  1.4 0.1 select_reduce_fusion
  1.5 0.6 compare_select_fusion.picks_ref
  2.1 201.8 %sample.1 = (bf16[56,16,448]{2,1,0:T(8,128)(2,1)}, f32[8,56,448]{2,1,0:T(8,128)}) custom-call(s32[2,56]{1,0:T(2,128)} %compare_select_fusion.picks_ref, bf16[2,448,1792]{2,1,0:T(8,128)(2,1)} %bitcast.2, bf16[448,3584]{1,0:T(8,128)(2,1)} %bitcast.3, bf16[2,3584,1792]{2,1,0:T(8,128)(2,1)} %kids_hbm.1, bf16[7168,3584]{1,0:T(8,128)(2,1)} %front_hbm.1), custom_call_target="tpu_custom_call" | custom-call | flops 46036680704 | bytes 102760448 | tf_op jit(solution)/shard_map/sample/pallas_call | solution.py:1056
  203.9 2.2 %copy.9 = bf16[56,16,448]{2,1,0:T(8,128)(2,1)} copy(bf16[56,16,448]{2,1,0:T(8,128)(2,1)} %get-tuple-element.6) | data formatting | bytes 1605632
  206.1 2.2 %copy.10 = f32[8,56,448]{2,1,0:T(8,128)} copy(f32[8,56,448]{2,1,0:T(8,128)} %get-tuple-element.7) | data formatting | bytes 1605632
  (2 shorter events, 0.0 us)
